TPU v7x, 32 devices: a whole 2x2x4 slice. The times are simulated.
32 devices in a mesh: dp: 16 (over z, y, core), tensor: 2 (over x).
Axes of the slice: x: 2, y: 2, z: 4, core: 2. Of those that a mesh axis runs over, the one named last changes fastest.
Arguments:
- inputs: bfloat16 [16384, 1536], P(('dp', 'tensor')), may hold values from -6 to 6
- gain_attn: bfloat16 [1536], P('dp'), may hold values from 0.5 to 1.5
- w_query: bfloat16 [1536, 1536], P('dp', 'tensor'), may hold values from -0.21875 to 0.21875
- w_key: bfloat16 [1536, 512], P('dp', 'tensor'), may hold values from -0.15625 to 0.15625
- w_value: bfloat16 [1536, 512], P('dp', 'tensor'), may hold values from -0.15625 to 0.15625
- w_out: bfloat16 [1536, 1536], P('tensor', 'dp'), may hold values from -1.25 to 1.25
- gain_moe: bfloat16 [1536], P('dp'), may hold values from 0.5 to 1.5
- w_router: bfloat16 [1536, 40], P('dp'), may hold values from -0.078125 to 0.078125
- w_gate: bfloat16 [40, 786432], P(None, ('dp', 'tensor')), may hold values from -0.15625 to 0.15625
- w_up: bfloat16 [40, 786432], P(None, ('dp', 'tensor')), may hold values from -0.15625 to 0.15625
- w_down: bfloat16 [40, 786432], P(None, ('dp', 'tensor')), may hold values from -0.5 to 0.5
- routes: int32 [16384, 8], P('dp'), may hold values from 0 to 39, all different within a row; in each aligned block of 1024 rows (0 to 1023, 1024 to 2047, ...) at most 256 rows name the same one
- cotangent: bfloat16 [16384, 1536], P(('dp', 'tensor')), may hold values from -6 to 6
Outputs:
- outputs: bfloat16 [16384, 1536], P(('dp', 'tensor'))
- input_grad: float32 [16384, 1536], P(('dp', 'tensor'))
- gain_attn_grad: float32 [1536], P('dp')
- w_query_grad: float32 [1536, 1536], P('dp', 'tensor')
- w_key_grad: float32 [1536, 512], P('dp', 'tensor')
- w_value_grad: float32 [1536, 512], P('dp', 'tensor')
- w_out_grad: float32 [1536, 1536], P('tensor', 'dp')
- gain_moe_grad: float32 [1536], P('dp')
- w_router_grad: float32 [1536, 40], P('dp')
- w_gate_grad: float32 [40, 786432], P(None, ('dp', 'tensor'))
- w_up_grad: float32 [40, 786432], P(None, ('dp', 'tensor'))
- w_down_grad: float32 [40, 786432], P(None, ('dp', 'tensor'))
Inputs may be any that keep to these rules, and one draw needn't show every extreme that they name: `routes`: each row names 8 different experts. Within one sequence's 1024 rows no expert is named by more than 256 rows, and in some sequence one expert is named by exactly 256 rows.
All inputs are finite; a program needn't handle non-finite values.
Results may differ from a plain program's by a relative error of at most 0.025.
Values may be sent and summed in bfloat16 or wider, within the bound.
A program may use at most 512 MiB of HBM per device.

v0:
```python
import functools

import jax
import jax.numpy as jnp
from jax import lax
from jax.experimental import pallas as pl
from jax.experimental.pallas import tpu as pltpu
from jax.sharding import PartitionSpec as P


D = 1536
HD = 64
E = 40
GROUPS = 5
RINGED = 5
TILES = 4
HOPS = (
    (),
    (),
    (),
    (),
    ((0, 1), (1, 1), (2, 1)),
    ((0, 1), (1, 1), (2, 1), (3, 1)),
    ((0, 1), (1, 1), (2, 1), (3, 1), (4, 1)),
    ((0, 1), (1, 1)),
    ((2, 1), (3, 2), (4, 3)),
)
BLOCK = 256
RING = (0, 2, 4, 6, 7, 5, 3, 1)


epsilon = 1e-06
contract_last = (((1,), (1,)), ((), ()))
contract_first = (((0,), (0,)), ((), ()))


def rope_tables(seq_len, width):
    position = jnp.arange(seq_len).astype(jnp.float32)
    freq = 10000.0 ** (-jnp.arange(width // 2).astype(jnp.float32) * 2.0 / width)
    angle = position[:, None] * freq[None, :]
    return (jnp.cos(angle)[:, None, :], jnp.sin(angle)[:, None, :])


def rotate(values, cosine, sine):
    half = values.shape[-1] // 2
    first_half = values[..., :half]
    second_half = values[..., half:]
    return jnp.concatenate(
        [first_half * cosine - second_half * sine, second_half * cosine + first_half * sine],
        axis=-1,
    )


def unrotate(grads, cosine, sine):
    half = grads.shape[-1] // 2
    first_half = grads[..., :half]
    second_half = grads[..., half:]
    return jnp.concatenate(
        [first_half * cosine + second_half * sine, second_half * cosine - first_half * sine],
        axis=-1,
    )


def rms_factor(values):
    return lax.rsqrt(jnp.mean(values * values, axis=-1, keepdims=True) + epsilon)


def norm_backward(values, factor, gain_f, normed_grad):
    weighted = normed_grad * gain_f
    values_grad = factor * weighted - values * factor**3 * jnp.mean(
        values * weighted, axis=-1, keepdims=True
    )
    return (values_grad, jnp.sum(normed_grad * values * factor, axis=0))


def block_scores(query_blk, key_rot, offset):
    rows, keys = query_blk.shape[0], key_rot.shape[0]
    scores = jnp.einsum(
        "qcgd,kcd->cgqk", query_blk, key_rot, preferred_element_type=jnp.float32
    ) * HD ** (-0.5)
    causal = (offset + jnp.arange(rows, dtype=jnp.int32))[:, None] >= jnp.arange(
        keys, dtype=jnp.int32
    )[None, :]
    return jnp.where(causal, scores, -1e30)


def attention_forward(query_rot, key_rot, value_hd):
    seq_len, heads, width = query_rot.shape
    kv_heads = key_rot.shape[1]
    block_rows = min(BLOCK, seq_len)
    grouped = query_rot.reshape(seq_len, kv_heads, heads // kv_heads, width)
    blocks = seq_len // block_rows
    half = max(1, blocks // 2)
    outs, logs = [None] * blocks, [None] * blocks
    for number in [block for first in range(half) for block in range(first, blocks, half)]:
        start, stop = number * block_rows, (number + 1) * block_rows
        scores = block_scores(grouped[start:stop], key_rot[:stop], start)
        highest_score = jnp.max(scores, axis=-1, keepdims=True)
        expo = jnp.exp(scores - highest_score)
        total = jnp.sum(expo, axis=-1, keepdims=True)
        prob_low = (expo / total).astype(jnp.bfloat16)
        attn_blk = jnp.einsum(
            "cgqk,kcd->qcgd", prob_low, value_hd[:stop], preferred_element_type=jnp.float32
        )
        outs[number] = attn_blk.astype(jnp.bfloat16).reshape(block_rows, heads * width)
        logs[number] = (highest_score + jnp.log(total))[..., 0]
        if number == blocks - half and half > 1:
            key_rot, value_hd, outs[0], outs[number] = lax.optimization_barrier(
                (key_rot, value_hd, outs[0], outs[number])
            )
    return outs, logs


def attention_backward(query_rot, key_rot, value_hd, logs, out_grad_all):
    seq_len, heads, width = query_rot.shape
    kv_heads = key_rot.shape[1]
    block_rows = min(BLOCK, seq_len)
    grouped = query_rot.reshape(seq_len, kv_heads, heads // kv_heads, width)
    grad_groups = out_grad_all.reshape(grouped.shape)
    query_grads = []
    key_acc = jnp.zeros((seq_len, kv_heads, width), jnp.float32)
    value_acc = key_acc
    for number, start in enumerate(range(0, seq_len, block_rows)):
        stop = start + block_rows
        query_blk, grad_blk = grouped[start:stop], grad_groups[start:stop]
        keys, values = key_rot[:stop], value_hd[:stop]
        scores = block_scores(query_blk, keys, start)
        attn_prob = jnp.exp(scores - logs[number][..., None])
        prob_low = attn_prob.astype(jnp.bfloat16)
        prob_grad = jnp.einsum(
            "qcgd,kcd->cgqk", grad_blk, values, preferred_element_type=jnp.float32
        )
        score_grad = (
            attn_prob * (prob_grad - jnp.sum(attn_prob * prob_grad, axis=-1, keepdims=True))
        ).astype(jnp.bfloat16)
        query_grad = jnp.einsum(
            "cgqk,kcd->qcgd", score_grad, keys, preferred_element_type=jnp.float32
        ) * HD ** (-0.5)
        key_part = jnp.einsum(
            "cgqk,qcgd->kcd", score_grad, query_blk, preferred_element_type=jnp.float32
        ) * HD ** (-0.5)
        value_part = jnp.einsum(
            "cgqk,qcgd->kcd", prob_low, grad_blk, preferred_element_type=jnp.float32
        )
        rest = ((0, seq_len - stop), (0, 0), (0, 0))
        key_acc = key_acc + jnp.pad(key_part, rest)
        value_acc = value_acc + jnp.pad(value_part, rest)
        query_grads.append(query_grad.reshape(block_rows, heads, width))
    return jnp.concatenate(query_grads, axis=0), key_acc, value_acc


def swap(values, axis):
    return lax.ppermute(values, axis, [(0, 1), (1, 0)])


def gather_ordered(values):
    if lax.axis_size("tensor") != 2:
        return lax.all_gather(values, "tensor", axis=0, tiled=True)
    other = swap(values, "tensor")
    first = lax.axis_index("tensor") == 0
    return jnp.concatenate(
        [jnp.where(first, values, other), jnp.where(first, other, values)], axis=0
    )


def gather_rows(values):
    if lax.axis_size("tensor") == 2:
        sequence = jnp.concatenate([values, swap(values, "tensor")], axis=0)
    else:
        sequence = lax.all_gather(values, "tensor", axis=0, tiled=True)
    return jnp.concatenate([sequence, swap(sequence, "core")], axis=0)


def scatter_tensor(values, ordered):
    if lax.axis_size("tensor") != 2:
        return lax.psum_scatter(values, "tensor", scatter_dimension=0, tiled=True).astype(
            jnp.float32
        )
    half = values.shape[0] // 2
    if ordered:
        first = lax.axis_index("tensor") == 0
        low, high = values[:half], values[half:]
        kept, given = jnp.where(first, low, high), jnp.where(first, high, low)
    else:
        kept, given = values[:half], values[half:]
    return kept.astype(jnp.float32) + swap(given, "tensor").astype(jnp.float32)


def scatter_rows(values):
    half = values.shape[0] // 2
    mine = values[:half].astype(jnp.float32) + swap(
        values[half:].astype(jnp.bfloat16), "core"
    ).astype(jnp.float32)
    return scatter_tensor(mine.astype(jnp.bfloat16), False)


def sequence_routes(routes, own_rows):
    if lax.axis_size("tensor") == 2:
        second = lax.axis_index("tensor") == 1
        low, high = routes[:own_rows], routes[own_rows:]
        routes = jnp.concatenate(
            [jnp.where(second, high, low), jnp.where(second, low, high)], axis=0
        )
    return jnp.concatenate([routes, swap(routes, "core")], axis=0)


def dense_gates(logits, routes):
    experts = jnp.arange(E, dtype=jnp.int32)
    used = jnp.any(routes[:, :, None] == experts[None, None, :], axis=1)
    top = jnp.max(jnp.where(used, logits, -jnp.inf), axis=-1, keepdims=True)
    expo = jnp.where(used, jnp.exp(jnp.minimum(logits - top, 0.0)), 0.0)
    return expo / jnp.sum(expo, axis=-1, keepdims=True)


class Ring:
    def __init__(self, grads, flip, starts):
        self.grads, self.step, self.hop_number = grads, -1 if flip else 1, 0
        self.count = len(RING)
        self.rows = grads.shape[2] // self.count
        self.starts = starts
        far = self.count // 2
        self.state = (self.own(self.step * far), self.own(-self.step * (far - 1)))

    def own(self, ahead):
        start = self.starts[ahead % self.count]
        return lax.dynamic_slice_in_dim(self.grads, start, self.rows, 2)

    def send(self, block, way):
        pairs = [(RING[i], RING[(i + way) % self.count]) for i in range(self.count)]
        return lax.ppermute(block, "chip", pairs)

    def hop(self):
        self.hop_number += 1
        hop, far = self.hop_number, self.count // 2
        ahead, behind = self.state
        ahead = self.send(ahead, self.step)
        if hop < far:
            ahead = self.add(ahead, self.own(self.step * (far - hop)))
        if hop < far - 1:
            behind = self.add(
                self.send(behind, -self.step), self.own(-self.step * (far - 1 - hop))
            )
        elif hop == far - 1:
            behind = self.send(behind, -self.step)
        self.state = (ahead, behind)

    def add(self, block, own):
        return (block.astype(jnp.float32) + own.astype(jnp.float32)).astype(jnp.bfloat16)

    def result(self):
        ahead, behind = self.state
        return (
            self.own(0).astype(jnp.float32)
            + ahead.astype(jnp.float32)
            + behind.astype(jnp.float32)
        )


class Whole:
    def __init__(self, grads):
        self.state = lax.psum_scatter(
            grads, "chip", scatter_dimension=2, tiled=True
        )

    def hop(self):
        pass

    def result(self):
        return self.state.astype(jnp.float32)


def ring_starts(rows):
    count = len(RING)
    if lax.axis_size("chip") != count:
        return None
    table = [[RING[(RING.index(c) + a) % count] * rows for a in range(count)] for c in range(count)]
    mine = jnp.asarray(table, jnp.int32)[lax.axis_index("chip")]
    return [mine[a] for a in range(count)]


def scatter_experts(grads, number, starts):
    if number < RINGED and starts is not None:
        return Ring(grads, number % 2 == 1, starts)
    return Whole(grads)


def run_hops(sums, stage):
    for which, count in HOPS[stage]:
        for _ in range(count):
            sums[which].hop()


def tie(values, sums):
    values, states = lax.optimization_barrier((values, [each.state for each in sums]))
    for each, state in zip(sums, states):
        each.state = state
    return values


def expert_kernel(first, core_ref, tokens_ref, cot_ref, gates_ref, weights_ref, *refs):
    if not first:
        mix_in, rows_in, *refs = refs
    mix_out, rows_out, gate_grad_ref, grads_ref, mix, rows, sums, in_sem, out_sem = refs
    step, steps = pl.program_id(0), pl.num_programs(0)
    size = tokens_ref.shape[0] // TILES
    width = tokens_ref.shape[1]
    gate_w, up_w, down_w = (weights_ref[k].reshape(-1, width) for k in range(3))
    pair = gate_w.shape[0]

    def arriving(tile, which):
        part = pl.ds(tile * size, size)
        source, target = ((mix_in, mix), (rows_in, rows))[which]
        return pltpu.make_async_copy(source.at[part], target.at[part], in_sem.at[which, tile])

    def leaving(tile, which):
        part = pl.ds(tile * size, size)
        source, target = ((mix, mix_out), (rows, rows_out))[which]
        return pltpu.make_async_copy(source.at[part], target.at[part], out_sem.at[which, tile])

    def dot(left, right, contract):
        return lax.dot_general(
            left, right, (contract, ((), ())), preferred_element_type=jnp.float32
        )

    if not first:

        @pl.when(step == 0)
        def _():
            for tile in range(TILES):
                arriving(tile, 0).start()
                arriving(tile, 1).start()

    sums[...] = jnp.zeros_like(sums)

    def one_tile(tile, carry):
        part = pl.ds(pl.multiple_of(tile * size, size), size)
        tokens, cot = tokens_ref[part, :], cot_ref[part, :]
        gate_h = dot(gate_w, tokens, ((1,), (1,)))
        up_h = dot(up_w, tokens, ((1,), (1,)))
        cot_h = dot(down_w, cot, ((1,), (1,)))
        gates = jnp.broadcast_to(
            gates_ref[0, :, part][:, None, :], (2, pair // 2, size)
        ).reshape(pair, size)
        sigma = jax.nn.sigmoid(gate_h)
        silu = gate_h * sigma
        hidden_h = silu * up_h
        gate_grad_ref[0, :, part] = jnp.sum((hidden_h * cot_h).reshape(2, pair // 2, size), axis=1)
        weighted = (gates * hidden_h).astype(jnp.bfloat16)
        hidden_grad = gates * cot_h
        gate_hg = (hidden_grad * up_h * (sigma + silu * (1.0 - sigma))).astype(jnp.bfloat16)
        up_hg = (hidden_grad * silu).astype(jnp.bfloat16)

        @pl.when(step == 0)
        def _():
            if first:
                mix[part, :] = jnp.zeros((size, width), jnp.float32)
                rows[part, :] = jnp.zeros((size, width), jnp.float32)
            else:
                arriving(tile, 0).wait()
                arriving(tile, 1).wait()

        mix[part, :] += dot(weighted, down_w, ((0,), (0,)))
        rows[part, :] += dot(gate_hg, gate_w, ((0,), (0,))) + dot(up_hg, up_w, ((0,), (0,)))
        sums[0] += dot(gate_hg, tokens, ((1,), (0,)))
        sums[1] += dot(up_hg, tokens, ((1,), (0,)))
        sums[2] += dot(weighted, cot, ((1,), (0,)))

        @pl.when(step == steps - 1)
        def _():
            leaving(tile, 0).start()
            leaving(tile, 1).start()

        return carry

    lax.fori_loop(0, TILES, one_tile, 0)
    grads_ref[...] = sums[...].astype(jnp.bfloat16).reshape(grads_ref.shape)

    @pl.when(step == steps - 1)
    def _():
        for tile in range(TILES):
            leaving(tile, 0).wait()
            leaving(tile, 1).wait()


def expert_call(tokens, cot, gates, gathered, totals):
    first = totals is None
    count, width = tokens.shape
    _, each, chips, _, shard, _ = gathered.shape
    pair = 2 * chips * shard
    core = lax.axis_index("core").astype(jnp.int32)[None]
    gates = gates.T.reshape(each // 2, 2, count)
    whole = pl.BlockSpec((count, width), lambda i, core: (0, 0), pipeline_mode=pl.Buffered(1))
    by_pair = pl.BlockSpec((1, 2, count), lambda i, core: (i, 0, 0))
    anywhere = pl.BlockSpec(memory_space=pl.ANY)
    total = jax.ShapeDtypeStruct((count, width), jnp.float32)
    mix, rows, gate_grad, grads = pl.pallas_call(
        functools.partial(expert_kernel, first),
        grid_spec=pltpu.PrefetchScalarGridSpec(
            num_scalar_prefetch=1,
            grid=(each // 2,),
            in_specs=[
                whole,
                whole,
                by_pair,
                pl.BlockSpec(
                    (3, 2, chips, None, shard, width), lambda i, core: (0, i, 0, core[0], 0, 0)
                ),
            ]
            + ([] if first else [anywhere, anywhere]),
            out_specs=[
                anywhere,
                anywhere,
                by_pair,
                pl.BlockSpec((3, 2, chips * shard, width), lambda i, core: (0, i, 0, 0)),
            ],
            scratch_shapes=[
                pltpu.VMEM((count, width), jnp.float32),
                pltpu.VMEM((count, width), jnp.float32),
                pltpu.VMEM((3, pair, width), jnp.float32),
                pltpu.SemaphoreType.DMA((2, TILES)),
                pltpu.SemaphoreType.DMA((2, TILES)),
            ],
        ),
        out_shape=[
            total,
            total,
            jax.ShapeDtypeStruct(gates.shape, jnp.float32),
            jax.ShapeDtypeStruct((3, each, chips * shard, width), jnp.bfloat16),
        ],
        input_output_aliases={} if first else {5: 0, 6: 1},
        compiler_params=pltpu.CompilerParams(vmem_limit_bytes=67043328),
        cost_estimate=pl.CostEstimate(
            flops=9 * count * width * pair * each,
            bytes_accessed=4 * 4 * count * width + 12 * each * chips * shard * width,
            transcendentals=count * pair * each // 2,
        ),
        name="experts",
    )(core, tokens, cot, gates, gathered, *(() if first else totals))
    return mix, rows, gate_grad.reshape(each, count).T, grads


def expert_group(tokens, cot, gates, gate_w, up_w, down_w):
    rows = tokens.shape[0]
    count, hidden = gate_w.shape[:2]
    flat = (count * hidden, D)
    gate_w, up_w, down_w = gate_w.reshape(flat), up_w.reshape(flat), down_w.reshape(flat)
    wide = jnp.broadcast_to(gates[:, :, None], (rows, count, hidden)).reshape(rows, -1)
    gate_h = lax.dot_general(tokens, gate_w, contract_last, preferred_element_type=jnp.float32)
    up_h = lax.dot_general(tokens, up_w, contract_last, preferred_element_type=jnp.float32)
    cot_h = lax.dot_general(cot, down_w, contract_last, preferred_element_type=jnp.float32)
    sigma = jax.nn.sigmoid(gate_h)
    silu = gate_h * sigma
    hidden_h = silu * up_h
    gate_grad = jnp.sum((hidden_h * cot_h).reshape(rows, count, hidden), axis=-1)
    hidden_grad = wide * cot_h
    weighted = (wide * hidden_h).astype(jnp.bfloat16)
    gate_hg = (hidden_grad * up_h * sigma * (1.0 + gate_h * (1.0 - sigma))).astype(jnp.bfloat16)
    up_hg = (hidden_grad * silu).astype(jnp.bfloat16)
    mixture = jnp.dot(weighted, down_w, preferred_element_type=jnp.float32)
    rows_grad = jnp.dot(gate_hg, gate_w, preferred_element_type=jnp.float32) + jnp.dot(
        up_hg, up_w, preferred_element_type=jnp.float32
    )
    grads = jnp.stack([
        lax.dot_general(left, right, contract_first, preferred_element_type=jnp.float32)
        .astype(jnp.bfloat16)
        .reshape(count, hidden, D)
        for left, right in ((gate_hg, tokens), (up_hg, tokens), (weighted, cot))
    ])
    return mixture, rows_grad, gate_grad, grads


def body(
    inputs,
    gain_attn,
    w_query,
    w_key,
    w_value,
    w_out,
    gain_moe,
    w_router,
    w_gate,
    w_up,
    w_down,
    routes,
    cotangent,
):
    parts = lax.axis_size("tensor")
    own_rows = inputs.shape[0]
    seq_len = own_rows * parts
    cosine, sine = rope_tables(seq_len, HD)
    inputs_f = inputs.astype(jnp.float32)
    q_cols, k_cols = w_query.shape[1], w_key.shape[1]
    proj_cols = q_cols + 2 * k_cols
    filler = jnp.zeros((w_query.shape[0], 127), jnp.bfloat16)
    packed = jnp.concatenate([w_query, w_key, w_value, gain_attn[:, None], filler], axis=1)
    packed = lax.all_gather(packed, ("chip", "core"), axis=0, tiled=True)
    proj_w, gain_one_f = packed[:, :proj_cols], packed[:, proj_cols].astype(jnp.float32)
    query_w, key_w, value_w = jnp.split(proj_w, [q_cols, q_cols + k_cols], axis=1)
    packed = jnp.concatenate(
        [w_out.T, w_router, gain_moe[:, None], filler[:, : 127 - E]], axis=1
    )
    packed, _ = lax.optimization_barrier((packed, proj_w))
    packed = lax.all_gather(packed, ("chip", "core"), axis=0, tiled=True)
    out_wt, router_w = packed[:, :q_cols], packed[:, q_cols : q_cols + E]
    gain_two_f = packed[:, q_cols + E].astype(jnp.float32)

    shard = w_gate.shape[1] // D
    starts = ring_starts(shard)
    groups = GROUPS
    each = E // groups
    stacked = [w.reshape(E, shard, D) for w in (w_gate, w_up, w_down)]
    gathered = []
    for g in range(groups):
        part = jnp.stack([w[g * each : (g + 1) * each] for w in stacked])
        gathered.append(lax.all_gather(part, ("chip", "core"), axis=2, tiled=True))

    inputs_all = gather_ordered(inputs)
    inputs_all, cot_later = lax.optimization_barrier((inputs_all, cotangent))
    cot_rows = gather_rows(cot_later)
    routes_rows = sequence_routes(routes, own_rows)

    scale_one = rms_factor(inputs_f)
    inputs_all = inputs_all.astype(jnp.float32)
    normed_all = (inputs_all * rms_factor(inputs_all) * gain_one_f).astype(jnp.bfloat16)
    query_proj = jnp.dot(normed_all, query_w, preferred_element_type=jnp.float32)
    key_proj = jnp.dot(normed_all, key_w, preferred_element_type=jnp.float32)
    value_proj = jnp.dot(normed_all, value_w, preferred_element_type=jnp.float32)
    query_rot = rotate(query_proj.reshape(seq_len, -1, HD), cosine, sine).astype(jnp.bfloat16)
    key_rot = rotate(key_proj.reshape(seq_len, -1, HD), cosine, sine).astype(jnp.bfloat16)
    value_hd = value_proj.reshape(seq_len, -1, HD).astype(jnp.bfloat16)
    attn_outs, log_total = attention_forward(query_rot, key_rot, value_hd)
    attn_out = jnp.concatenate(attn_outs, axis=0)
    chunks = len(attn_outs) // 2 if parts == 2 else 1
    piece = own_rows // chunks
    hidden_parts, scale_parts, normed_parts = [], [], []
    for c in range(chunks):
        both = jnp.concatenate([attn_outs[c], attn_outs[c + chunks]], axis=0) if parts == 2 else attn_out
        hidden_part = inputs_f[c * piece : (c + 1) * piece] + scatter_tensor(
            lax.dot_general(
                both, out_wt, contract_last, preferred_element_type=jnp.float32
            ).astype(jnp.bfloat16),
            True,
        )
        scale_part = rms_factor(hidden_part)
        hidden_parts.append(hidden_part)
        scale_parts.append(scale_part)
        normed_parts.append((hidden_part * scale_part * gain_two_f).astype(jnp.bfloat16))
    hidden_mid = jnp.concatenate(hidden_parts, axis=0)
    scale_two = jnp.concatenate(scale_parts, axis=0)
    normed_two = jnp.concatenate(normed_parts, axis=0)
    if parts == 2:
        sequence = jnp.concatenate(
            normed_parts + [swap(part, "tensor") for part in normed_parts], axis=0
        )
        token_rows = jnp.concatenate([sequence, swap(sequence, "core")], axis=0)
    else:
        token_rows = gather_rows(normed_two)
    logits = jnp.dot(token_rows, router_w, preferred_element_type=jnp.float32)
    gates = dense_gates(logits, routes_rows)

    mixture, rows_grad, gate_grads, expert_sums = 0.0, 0.0, [], []
    for g in range(groups):
        token_rows_g, cot_rows_g = token_rows, cot_rows
        if g > 0:
            run_hops(expert_sums, g - 1)
            token_rows_g, cot_rows_g, mixture, rows_grad, grads, gathered[g] = tie(
                (token_rows, cot_rows, mixture, rows_grad, grads, gathered[g]),
                [expert_sums[done] for done, _ in HOPS[g - 1]],
            )
            expert_sums.append(scatter_experts(grads, g - 1, starts))
        by_core = gathered[g].reshape(3, each, -1, 2, shard, D)
        group_gates = gates[:, g * each : (g + 1) * each]
        if shard == 16 and by_core.shape[2] == 8:
            mixture, rows_grad, gate_grad, grads = expert_call(
                token_rows_g,
                cot_rows_g,
                group_gates,
                by_core,
                (mixture, rows_grad) if g > 0 else None,
            )
        else:
            by_core = lax.dynamic_index_in_dim(by_core, lax.axis_index("core"), 3, keepdims=False)
            gate_w, up_w, down_w = by_core.reshape(3, each, -1, D)
            mix, rows, gate_grad, grads = expert_group(
                token_rows_g, cot_rows_g, group_gates, gate_w, up_w, down_w
            )
            mixture, rows_grad = mixture + mix, rows_grad + rows
        gate_grads.append(gate_grad)
    run_hops(expert_sums, groups - 1)
    mixture, rows_grad, grads = tie(
        (mixture, rows_grad, grads), [expert_sums[done] for done, _ in HOPS[groups - 1]]
    )
    expert_sums.append(scatter_experts(grads, groups - 1, starts))
    gate_grad_own = scatter_rows(jnp.concatenate(gate_grads, axis=1))
    if parts == 2:
        probs_own = gates[:own_rows]
    else:
        probs_own = lax.dynamic_slice_in_dim(
            gates, lax.axis_index("tensor") * own_rows, own_rows, 0
        )
    logit_grad = (
        probs_own * (gate_grad_own - jnp.sum(probs_own * gate_grad_own, axis=-1, keepdims=True))
    ).astype(jnp.bfloat16)
    router_part = lax.dot_general(
        logit_grad, router_w, contract_last, preferred_element_type=jnp.float32
    )
    router_grad = lax.dot_general(
        normed_two,
        jnp.pad(logit_grad, ((0, 0), (0, 128 - E))),
        contract_first,
        preferred_element_type=jnp.float32,
    )
    half_rows = seq_len
    mine = rows_grad[:half_rows] + swap(
        rows_grad[half_rows:].astype(jnp.bfloat16), "core"
    ).astype(jnp.float32)
    mid_parts, gain_two_grad = [], 0.0
    for c in range(chunks):
        part = slice(c * piece, (c + 1) * piece)
        if parts == 2:
            given = mine[own_rows + c * piece : own_rows + (c + 1) * piece]
            summed = mine[part] + swap(given.astype(jnp.bfloat16), "tensor").astype(jnp.float32)
        else:
            summed = scatter_tensor(mine.astype(jnp.bfloat16), False)
        mid_part, gain_part = norm_backward(
            hidden_mid[part], scale_two[part], gain_two_f, summed + router_part[part]
        )
        mid_parts.append(cotangent[part].astype(jnp.float32) + mid_part)
        gain_two_grad = gain_two_grad + gain_part
    mid_grad = jnp.concatenate(mid_parts, axis=0)
    if parts == 2:
        own_low = [part.astype(jnp.bfloat16) for part in mid_parts]
        other = jnp.concatenate([swap(part, "tensor") for part in own_low], axis=0)
        own_low = jnp.concatenate(own_low, axis=0)
        first = lax.axis_index("tensor") == 0
        mid_all = jnp.concatenate(
            [jnp.where(first, own_low, other), jnp.where(first, other, own_low)], axis=0
        )
    else:
        mid_all = gather_ordered(mid_grad.astype(jnp.bfloat16))
    run_hops(expert_sums, groups)
    mid_all, mixture = tie((mid_all, mixture), expert_sums)
    outputs = (hidden_mid + scatter_rows(mixture)).astype(jnp.bfloat16)
    out_wt_grad = lax.dot_general(
        mid_all, attn_out, contract_first, preferred_element_type=jnp.float32
    )
    column = jnp.arange(128, dtype=jnp.int32)[None, :]
    early = jnp.concatenate(
        [
            out_wt_grad.astype(jnp.bfloat16),
            jnp.where(column == E + 1, gain_two_grad[:, None], router_grad).astype(jnp.bfloat16),
        ],
        axis=1,
    )
    early = lax.psum_scatter(early, ("chip", "core"), scatter_dimension=0, tiled=True).astype(
        jnp.float32
    )
    attn_out_grad = jnp.dot(mid_all, out_wt, preferred_element_type=jnp.float32).astype(
        jnp.bfloat16
    )
    query_grad, key_grad, value_grad = attention_backward(
        query_rot, key_rot, value_hd, log_total, attn_out_grad
    )
    run_hops(expert_sums, groups + 1)
    query_grad, key_grad, value_grad = tie((query_grad, key_grad, value_grad), expert_sums)
    query_pg = unrotate(query_grad, cosine, sine).reshape(seq_len, -1).astype(jnp.bfloat16)
    key_pg = unrotate(key_grad, cosine, sine).reshape(seq_len, -1).astype(jnp.bfloat16)
    value_pg = value_grad.reshape(seq_len, -1).astype(jnp.bfloat16)
    proj_pg = jnp.concatenate([query_pg, key_pg, value_pg], axis=1)
    proj_w_grad = lax.dot_general(
        normed_all, proj_pg, contract_first, preferred_element_type=jnp.float32
    )
    normed_one_grad = scatter_tensor(
        lax.dot_general(
            proj_pg, proj_w, contract_last, preferred_element_type=jnp.float32
        ).astype(jnp.bfloat16),
        True,
    )
    input_part, gain_one_grad = norm_backward(inputs_f, scale_one, gain_one_f, normed_one_grad)
    input_grad = mid_grad + input_part
    late = jnp.concatenate(
        [
            proj_w_grad.astype(jnp.bfloat16),
            jnp.where(column == E, gain_one_grad[:, None], 0.0).astype(jnp.bfloat16),
        ],
        axis=1,
    )
    run_hops(expert_sums, groups + 2)
    late = tie(late, expert_sums)
    late = lax.psum_scatter(late, ("chip", "core"), scatter_dimension=0, tiled=True).astype(
        jnp.float32
    )
    run_hops(expert_sums, groups + 3)
    shared = early[:, q_cols:] + late[:, proj_cols:]
    if parts == 2:
        shared = shared + swap(shared, "tensor")
    else:
        shared = lax.psum(shared, "tensor")
    expert_grads = jnp.concatenate([each.result() for each in expert_sums], axis=1)
    expert_grads = expert_grads.reshape(3, E, shard * D)
    return (
        outputs,
        input_grad,
        shared[:, E],
        late[:, :q_cols],
        late[:, q_cols : q_cols + k_cols],
        late[:, q_cols + k_cols : proj_cols],
        early[:, :q_cols].T,
        shared[:, E + 1],
        shared[:, :E],
        expert_grads[0],
        expert_grads[1],
        expert_grads[2],
    )


def solution(mesh):
    dp, parts = mesh.devices.shape
    cores = jax.sharding.Mesh(mesh.devices.reshape(dp // 2, 2, parts), ("chip", "core", "tensor"))
    dp = ("chip", "core")
    every = ("chip", "core", "tensor")
    in_specs = (
        P(every, None),
        P(dp),
        P(dp, "tensor"),
        P(dp, "tensor"),
        P(dp, "tensor"),
        P("tensor", dp),
        P(dp),
        P(dp, None),
        P(None, every),
        P(None, every),
        P(None, every),
        P(dp, None),
        P(every, None),
    )
    out_specs = (
        P(every, None),
        P(every, None),
        P(dp),
        P(dp, "tensor"),
        P(dp, "tensor"),
        P(dp, "tensor"),
        P("tensor", dp),
        P(dp),
        P(dp, None),
        P(None, every),
        P(None, every),
        P(None, every),
    )

    return jax.shard_map(body, mesh=cores, in_specs=in_specs, out_specs=out_specs, check_vma=False)
```

profile of v0, /device:TPU:0, one launch (start us, length us, event | category | flops | bytes accessed | tf_op | source)
XLA Modules:
  0.0 1416.9 jit_solution(17962818457103331906)
XLA Ops:
  33.2 31.3 %collective-permute-done = bf16[512,1536]{1,0:T(8,128)(2,1)} collective-permute-done((bf16[512,1536]{1,0:T(8,128)(2,1)S(1)}, bf16[512,1536]{1,0:T(8,128)(2,1)}, u32[]{:S(2)}, u32[]{:S(2)}) %collective-permute-start) | collective-permute-done | bytes 1572896 | tf_op jit(solution)/shard_map/ppermute | solution.py:153
  95.2 13.8 all-gather.10.cloned.1.call-done
  138.2 14.3 %collective-permute-done.2 = bf16[256,1536]{1,0:T(8,128)(2,1)} collective-permute-done((bf16[256,1536]{1,0:T(8,128)(2,1)}, bf16[256,1536]{1,0:T(8,128)(2,1)}, u32[]{:S(2)}, u32[]{:S(2)}) %collective-permute-start.2) | collective-permute-done | bytes 786464 | tf_op jit(solution)/shard_map/ppermute | solution.py:153
  177.9 15.1 %collective-permute-done.4 = bf16[256,1536]{1,0:T(8,128)(2,1)} collective-permute-done((bf16[256,1536]{1,0:T(8,128)(2,1)}, bf16[256,1536]{1,0:T(8,128)(2,1)}, u32[]{:S(2)}, u32[]{:S(2)}) %collective-permute-start.4) | collective-permute-done | bytes 786464 | tf_op jit(solution)/shard_map/ppermute | solution.py:153
  225.5 80.3 %experts.5 = (f32[2048,1536]{1,0:T(8,128)}, f32[2048,1536]{1,0:T(8,128)}, f32[4,2,2048]{2,1,0:T(2,128)}, bf16[3,8,128,1536]{3,2,1,0:T(8,128)(2,1)}) custom-call(s32[1]{0:T(128)} %bitcast.40.core_ref, bf16[2048,1536]{1,0:T(8,128)(2,1)} %copy-done.20, bf16[2048,1536]{1,0:T(8,128)(2,1)} %copy-done.103, f32[4,2,2048]{2,1,0:T(2,128)} %reshape.393.gates_ref, ...), custom_call_target="tpu_custom_call" | custom-call | flops 57982058496 | bytes 69206016 | tf_op jit(solution)/shard_map/experts/pallas_call | solution.py:396
  308.6 79.7 %experts.6 = (f32[2048,1536]{1,0:T(8,128)}, f32[2048,1536]{1,0:T(8,128)}, f32[4,2,2048]{2,1,0:T(2,128)}, bf16[3,8,128,1536]{3,2,1,0:T(8,128)(2,1)}) custom-call(s32[1]{0:T(128)} %bitcast.40.core_ref, bf16[2048,1536]{1,0:T(8,128)(2,1)} %copy-done.20, bf16[2048,1536]{1,0:T(8,128)(2,1)} %copy-done.103, ...), custom_call_target="tpu_custom_call", output_to_operand_aliasing={{0}: (5, {}), {1}: (6, {})} | custom-call | flops 57982058496 | bytes 69206016 | tf_op jit(solution)/shard_map/experts/pallas_call | solution.py:396
  389.8 19.1 %all-gather.16.cloned.1.call-done = bf16[3,8,256,1536]{3,2,1,0:T(8,128)(2,1)} async-done(((bf16[3,8,16,1536]{3,2,1,0:T(8,128)(2,1)}), bf16[3,8,256,1536]{3,2,1,0:T(8,128)(2,1)}) %all-gather.16.cloned.1.call-update) | async-done | bytes 18874384 | tf_op jit(solution)/shard_map/all_gather | solution.py:515
  408.9 79.3 %experts.7 = (f32[2048,1536]{1,0:T(8,128)}, f32[2048,1536]{1,0:T(8,128)}, f32[4,2,2048]{2,1,0:T(2,128)}, bf16[3,8,128,1536]{3,2,1,0:T(8,128)(2,1)}) custom-call(s32[1]{0:T(128)} %bitcast.40.core_ref, bf16[2048,1536]{1,0:T(8,128)(2,1)} %copy-done.20, bf16[2048,1536]{1,0:T(8,128)(2,1)} %copy-done.103, ...), custom_call_target="tpu_custom_call", output_to_operand_aliasing={{0}: (5, {}), {1}: (6, {})} | custom-call | flops 57982058496 | bytes 69206016 | tf_op jit(solution)/shard_map/experts/pallas_call | solution.py:396
  488.2 21.0 %all-gather.18.cloned.1.call-done = bf16[3,8,256,1536]{3,2,1,0:T(8,128)(2,1)} async-done(((bf16[3,8,16,1536]{3,2,1,0:T(8,128)(2,1)}), bf16[3,8,256,1536]{3,2,1,0:T(8,128)(2,1)}) %all-gather.18.cloned.1.call-update) | async-done | bytes 18874384 | tf_op jit(solution)/shard_map/all_gather | solution.py:515
  509.2 79.6 %experts.8 = (f32[2048,1536]{1,0:T(8,128)}, f32[2048,1536]{1,0:T(8,128)}, f32[4,2,2048]{2,1,0:T(2,128)}, bf16[3,8,128,1536]{3,2,1,0:T(8,128)(2,1)}) custom-call(s32[1]{0:T(128)} %bitcast.40.core_ref, bf16[2048,1536]{1,0:T(8,128)(2,1)} %copy-done.20, bf16[2048,1536]{1,0:T(8,128)(2,1)} %copy-done.103, ...), custom_call_target="tpu_custom_call", output_to_operand_aliasing={{0}: (5, {}), {1}: (6, {})} | custom-call | flops 57982058496 | bytes 69206016 | tf_op jit(solution)/shard_map/experts/pallas_call | solution.py:396
  590.4 19.3 %all-gather.20.cloned.1.call-done = bf16[3,8,256,1536]{3,2,1,0:T(8,128)(2,1)} async-done(((bf16[3,8,16,1536]{3,2,1,0:T(8,128)(2,1)}), bf16[3,8,256,1536]{3,2,1,0:T(8,128)(2,1)}) %all-gather.20.cloned.1.call-update) | async-done | bytes 18874384 | tf_op jit(solution)/shard_map/all_gather | solution.py:515
  609.7 79.3 %experts.9 = (f32[2048,1536]{1,0:T(8,128)}, f32[2048,1536]{1,0:T(8,128)}, f32[4,2,2048]{2,1,0:T(2,128)}, bf16[3,8,128,1536]{3,2,1,0:T(8,128)(2,1)}) custom-call(s32[1]{0:T(128)} %bitcast.40.core_ref, bf16[2048,1536]{1,0:T(8,128)(2,1)} %copy-done.20, bf16[2048,1536]{1,0:T(8,128)(2,1)} %copy-done.103, ...), custom_call_target="tpu_custom_call", output_to_operand_aliasing={{0}: (5, {}), {1}: (6, {})} | custom-call | flops 57982058496 | bytes 69206016 | tf_op jit(solution)/shard_map/experts/pallas_call | solution.py:396
  711.9 11.6 collective-permute-done.10
  730.1 18.6 %collective-permute-done.14 = bf16[3,8,16,1536]{3,2,1,0:T(8,128)(2,1)} collective-permute-done((bf16[3,8,16,1536]{3,2,1,0:T(8,128)(2,1)}, bf16[3,8,16,1536]{3,2,1,0:T(8,128)(2,1)}, u32[]{:S(2)}, u32[]{:S(2)}) %collective-permute-start.14) | collective-permute-done | bytes 1179680 | tf_op jit(solution)/shard_map/ppermute | solution.py:230
  748.7 25.4 %collective-permute-done.13 = bf16[3,8,16,1536]{3,2,1,0:T(8,128)(2,1)} collective-permute-done((bf16[3,8,16,1536]{3,2,1,0:T(8,128)(2,1)}, bf16[3,8,16,1536]{3,2,1,0:T(8,128)(2,1)}, u32[]{:S(2)}, u32[]{:S(2)}) %collective-permute-start.13) | collective-permute-done | bytes 1179680 | tf_op jit(solution)/shard_map/ppermute | solution.py:230
  807.0 13.8 collective-permute-done.29
  830.2 16.5 %collective-permute-done.23 = bf16[3,8,16,1536]{3,2,1,0:T(8,128)(2,1)} collective-permute-done((bf16[3,8,16,1536]{3,2,1,0:T(8,128)(2,1)}, bf16[3,8,16,1536]{3,2,1,0:T(8,128)(2,1)}, u32[]{:S(2)}, u32[]{:S(2)}) %collective-permute-start.23) | collective-permute-done | bytes 1179680 | tf_op jit(solution)/shard_map/ppermute | solution.py:230
  854.2 16.5 %collective-permute-done.27 = bf16[3,8,16,1536]{3,2,1,0:T(8,128)(2,1)S(1)} collective-permute-done((bf16[3,8,16,1536]{3,2,1,0:T(8,128)(2,1)}, bf16[3,8,16,1536]{3,2,1,0:T(8,128)(2,1)S(1)}, u32[]{:S(2)}, u32[]{:S(2)}) %collective-permute-start.27) | collective-permute-done | bytes 1179680 | tf_op jit(solution)/shard_map/ppermute | solution.py:230
  872.2 23.6 %collective-permute-done.26 = bf16[3,8,16,1536]{3,2,1,0:T(8,128)(2,1)} collective-permute-done((bf16[3,8,16,1536]{3,2,1,0:T(8,128)(2,1)}, bf16[3,8,16,1536]{3,2,1,0:T(8,128)(2,1)}, u32[]{:S(2)}, u32[]{:S(2)}) %collective-permute-start.26) | collective-permute-done | bytes 1179680 | tf_op jit(solution)/shard_map/ppermute | solution.py:230
  914.5 10.8 collective-permute-done.20
  925.3 15.0 %collective-permute-done.21 = bf16[256,1536]{1,0:T(8,128)(2,1)S(1)} collective-permute-done((bf16[256,1536]{1,0:T(8,128)(2,1)S(1)}, bf16[256,1536]{1,0:T(8,128)(2,1)S(1)}, u32[]{:S(2)}, u32[]{:S(2)}) %collective-permute-start.21) | collective-permute-done | bytes 786464 | tf_op jit(solution)/shard_map/ppermute | solution.py:153
  952.4 10.4 fusion.9
  1025.4 8.0 fusion.74
  1049.6 23.7 %collective-permute-done.36 = bf16[3,8,16,1536]{3,2,1,0:T(8,128)(2,1)} collective-permute-done((bf16[3,8,16,1536]{3,2,1,0:T(8,128)(2,1)}, bf16[3,8,16,1536]{3,2,1,0:T(8,128)(2,1)}, u32[]{:S(2)}, u32[]{:S(2)}) %collective-permute-start.36) | collective-permute-done | bytes 1179680 | tf_op jit(solution)/shard_map/ppermute | solution.py:230
  1081.7 24.3 %collective-permute-done.39 = bf16[3,8,16,1536]{3,2,1,0:T(8,128)(2,1)} collective-permute-done((bf16[3,8,16,1536]{3,2,1,0:T(8,128)(2,1)}, bf16[3,8,16,1536]{3,2,1,0:T(8,128)(2,1)}, u32[]{:S(2)}, u32[]{:S(2)}) %collective-permute-start.39) | collective-permute-done | bytes 1179680 | tf_op jit(solution)/shard_map/ppermute | solution.py:230
  1115.1 16.0 %collective-permute-done.40 = bf16[3,8,16,1536]{3,2,1,0:T(8,128)(2,1)S(1)} collective-permute-done((bf16[3,8,16,1536]{3,2,1,0:T(8,128)(2,1)S(1)}, bf16[3,8,16,1536]{3,2,1,0:T(8,128)(2,1)S(1)}, u32[]{:S(2)}, u32[]{:S(2)}) %collective-permute-start.40) | collective-permute-done | bytes 1179680 | tf_op jit(solution)/shard_map/ppermute | solution.py:230
  1135.9 17.9 %collective-permute-done.35 = bf16[3,8,16,1536]{3,2,1,0:T(8,128)(2,1)S(1)} collective-permute-done((bf16[3,8,16,1536]{3,2,1,0:T(8,128)(2,1)S(1)}, bf16[3,8,16,1536]{3,2,1,0:T(8,128)(2,1)S(1)}, u32[]{:S(2)}, u32[]{:S(2)}) %collective-permute-start.35) | collective-permute-done | bytes 1179680 | tf_op jit(solution)/shard_map/ppermute | solution.py:230
  1183.9 16.7 %collective-permute-done.42 = bf16[512,1536]{1,0:T(8,128)(2,1)S(1)} collective-permute-done((bf16[512,1536]{1,0:T(8,128)(2,1)}, bf16[512,1536]{1,0:T(8,128)(2,1)S(1)}, u32[]{:S(2)}, u32[]{:S(2)}) %collective-permute-start.42) | collective-permute-done | bytes 1572896 | tf_op jit(solution)/shard_map/ppermute | solution.py:153
  1237.1 79.1 %collective-permute-done.50 = bf16[3,8,16,1536]{3,2,1,0:T(8,128)(2,1)} collective-permute-done((bf16[3,8,16,1536]{3,2,1,0:T(8,128)(2,1)}, bf16[3,8,16,1536]{3,2,1,0:T(8,128)(2,1)}, u32[]{:S(2)}, u32[]{:S(2)}) %collective-permute-start.50) | collective-permute-done | bytes 1179680 | tf_op jit(solution)/shard_map/ppermute | solution.py:230
  1332.9 12.9 collective-permute-done.51
  1359.9 16.8 %collective-permute-done.54 = bf16[3,8,16,1536]{3,2,1,0:T(8,128)(2,1)S(1)} collective-permute-done((bf16[3,8,16,1536]{3,2,1,0:T(8,128)(2,1)S(1)}, bf16[3,8,16,1536]{3,2,1,0:T(8,128)(2,1)S(1)}, u32[]{:S(2)}, u32[]{:S(2)}) %collective-permute-start.54) | collective-permute-done | bytes 1179680 | tf_op jit(solution)/shard_map/ppermute | solution.py:230
  1380.2 7.8 fusion.169
  (671 shorter events, 467.3 us)
Async XLA Ops:
  7.2 65.4 %all-gather.8.cloned.1.call-start = ((), (), s32[]{:S(2)}) async-start(), calls=%async_computation.2 | async-start | bytes 4595712 | tf_op jit(solution)/shard_map/all_gather | solution.py:496
  9.8 99.2 %all-gather.10.cloned.1.call-start = ((), (), s32[]{:S(2)}) async-start(), calls=%async_computation.3 | async-start | bytes 2924544 | tf_op jit(solution)/shard_map/all_gather | solution.py:503
  13.3 212.2 %all-gather.12.cloned.1.call-start = ((), (), s32[]{:S(2)}) async-start(), calls=%async_computation.4 | async-start | bytes 20054016 | tf_op jit(solution)/shard_map/all_gather | solution.py:515
  19.9 288.6 %all-gather.14.cloned.1.call-start = ((), (), s32[]{:S(2)}) async-start(), calls=%async_computation.5 | async-start | bytes 20054016 | tf_op jit(solution)/shard_map/all_gather | solution.py:515
  22.6 386.3 %all-gather.16.cloned.1.call-start = ((), (), s32[]{:S(2)}) async-start(), calls=%async_computation.6 | async-start | bytes 20054016 | tf_op jit(solution)/shard_map/all_gather | solution.py:515
  24.3 484.9 %all-gather.18.cloned.1.call-start = ((), (), s32[]{:S(2)}) async-start(), calls=%async_computation.7 | async-start | bytes 20054016 | tf_op jit(solution)/shard_map/all_gather | solution.py:515
  27.0 582.7 %all-gather.20.cloned.1.call-start = ((), (), s32[]{:S(2)}) async-start(), calls=%async_computation.8 | async-start | bytes 20054016 | tf_op jit(solution)/shard_map/all_gather | solution.py:515
  31.6 1298.5 %reduce-scatter.7.cloned.1.call-start = ((), (), s32[]{:S(2)}) async-start(), calls=%async_computation.9 | async-start | bytes 2924544
  70.8 62.5 %collective-permute-start.6 = (bf16[512,1536]{1,0:T(8,128)(2,1)S(1)}, bf16[512,1536]{1,0:T(8,128)(2,1)}, u32[]{:S(2)}, u32[]{:S(2)}) collective-permute-start(bf16[512,1536]{1,0:T(8,128)(2,1)S(1)} %copy-done.21), channel_id=1, source_target_pairs={{0,1},{1,0},{2,3},{3,2},{4,5},{5,4},{6,7},{7,6},{8,9},{9,8},{10,11... | collective-permute-start | bytes 4718600 | tf_op jit(solution)/shard_map/ppermute | solution.py:153
  136.7 60.8 %collective-permute-start.7 = (bf16[1024,1536]{1,0:T(8,128)(2,1)}, bf16[1024,1536]{1,0:T(8,128)(2,1)}, u32[]{:S(2)}, u32[]{:S(2)}) collective-permute-start(bf16[1024,1536]{1,0:T(8,128)(2,1)} %pad_maximum_fusion.3), channel_id=1, source_target_pairs={{0,2},{2,0},{1,3},{3,1},{4,6},{6,4},{5,7},{7,5},{8,10},{10,8},{9,1... | collective-permute-start | bytes 9437192 | tf_op jit(solution)/shard_map/ppermute | solution.py:153
  699.2 80.5 %collective-permute-start.12 = (bf16[3,8,16,1536]{3,2,1,0:T(8,128)(2,1)S(1)}, bf16[3,8,16,1536]{3,2,1,0:T(8,128)(2,1)}, u32[]{:S(2)}, u32[]{:S(2)}) collective-permute-start(bf16[3,8,16,1536]{3,2,1,0:T(8,128)(2,1)S(1)} %get-tuple-element.305), channel_id=1, source_target_pairs={{0,8},{8,16},{16,24},{24,28},{28,20},{20,12},{12,4},{4,0},{1,9},{9... | collective-permute-start | bytes 3538952 | tf_op jit(solution)/shard_map/ppermute | solution.py:230
  705.9 68.2 %collective-permute-start.13 = (bf16[3,8,16,1536]{3,2,1,0:T(8,128)(2,1)}, bf16[3,8,16,1536]{3,2,1,0:T(8,128)(2,1)}, u32[]{:S(2)}, u32[]{:S(2)}) collective-permute-start(bf16[3,8,16,1536]{3,2,1,0:T(8,128)(2,1)} %get-tuple-element.302), channel_id=1, source_target_pairs={{0,8},{8,16},{16,24},{24,28},{28,20},{20,12},{12,4},{4,0},{1,9},{9... | collective-permute-start | bytes 3538952 | tf_op jit(solution)/shard_map/ppermute | solution.py:230
  723.5 56.2 %collective-permute-start.11 = (bf16[3,8,16,1536]{3,2,1,0:T(8,128)(2,1)S(1)}, bf16[3,8,16,1536]{3,2,1,0:T(8,128)(2,1)S(1)}, u32[]{:S(2)}, u32[]{:S(2)}) collective-permute-start(bf16[3,8,16,1536]{3,2,1,0:T(8,128)(2,1)S(1)} %get-tuple-element.306), channel_id=1, source_target_pairs={{0,4},{8,0},{16,8},{24,16},{28,24},{20,28},{12,20},{4,12},{1,5},{9... | collective-permute-start | bytes 3538952 | tf_op jit(solution)/shard_map/ppermute | solution.py:230
  820.8 86.1 %collective-permute-start.25 = (bf16[3,8,16,1536]{3,2,1,0:T(8,128)(2,1)}, bf16[3,8,16,1536]{3,2,1,0:T(8,128)(2,1)}, u32[]{:S(2)}, u32[]{:S(2)}) collective-permute-start(bf16[3,8,16,1536]{3,2,1,0:T(8,128)(2,1)} %get-tuple-element.163), channel_id=1, source_target_pairs={{0,8},{8,16},{16,24},{24,28},{28,20},{20,12},{12,4},{4,0},{1,9},{9... | collective-permute-start | bytes 3538952 | tf_op jit(solution)/shard_map/ppermute | solution.py:230
  821.3 49.3 %collective-permute-start.27 = (bf16[3,8,16,1536]{3,2,1,0:T(8,128)(2,1)}, bf16[3,8,16,1536]{3,2,1,0:T(8,128)(2,1)S(1)}, u32[]{:S(2)}, u32[]{:S(2)}) collective-permute-start(bf16[3,8,16,1536]{3,2,1,0:T(8,128)(2,1)} %get-tuple-element.165), channel_id=1, source_target_pairs={{0,4},{8,0},{16,8},{24,16},{28,24},{20,28},{12,20},{4,12},{1,5},{9... | collective-permute-start | bytes 3538952 | tf_op jit(solution)/shard_map/ppermute | solution.py:230
  825.5 70.3 %collective-permute-start.26 = (bf16[3,8,16,1536]{3,2,1,0:T(8,128)(2,1)}, bf16[3,8,16,1536]{3,2,1,0:T(8,128)(2,1)}, u32[]{:S(2)}, u32[]{:S(2)}) collective-permute-start(bf16[3,8,16,1536]{3,2,1,0:T(8,128)(2,1)} %get-tuple-element.164), channel_id=1, source_target_pairs={{0,8},{8,16},{16,24},{24,28},{28,20},{20,12},{12,4},{4,0},{1,9},{9... | collective-permute-start | bytes 3538952 | tf_op jit(solution)/shard_map/ppermute | solution.py:230
  846.7 54.2 %collective-permute-start.19 = (bf16[256,1536]{1,0:T(8,128)(2,1)S(1)}, bf16[256,1536]{1,0:T(8,128)(2,1)S(1)}, u32[]{:S(2)}, u32[]{:S(2)}) collective-permute-start(bf16[256,1536]{1,0:T(8,128)(2,1)S(1)} %get-tuple-element.317), channel_id=1, source_target_pairs={{0,1},{1,0},{2,3},{3,2},{4,5},{5,4},{6,7},{7,6},{8,9},{9,8},{10,11... | collective-permute-start | bytes 2359304 | tf_op jit(solution)/shard_map/ppermute | solution.py:153
  848.2 52.7 %collective-permute-start.16 = (bf16[256,1536]{1,0:T(8,128)(2,1)S(1)}, bf16[256,1536]{1,0:T(8,128)(2,1)S(1)}, u32[]{:S(2)}, u32[]{:S(2)}) collective-permute-start(bf16[256,1536]{1,0:T(8,128)(2,1)S(1)} %get-tuple-element.318), channel_id=1, source_target_pairs={{0,1},{1,0},{2,3},{3,2},{4,5},{5,4},{6,7},{7,6},{8,9},{9,8},{10,11... | collective-permute-start | bytes 2359304 | tf_op jit(solution)/shard_map/ppermute | solution.py:153
  1013.5 59.8 %collective-permute-start.36 = (bf16[3,8,16,1536]{3,2,1,0:T(8,128)(2,1)}, bf16[3,8,16,1536]{3,2,1,0:T(8,128)(2,1)}, u32[]{:S(2)}, u32[]{:S(2)}) collective-permute-start(bf16[3,8,16,1536]{3,2,1,0:T(8,128)(2,1)} %get-tuple-element.174), channel_id=1, source_target_pairs={{0,8},{8,16},{16,24},{24,28},{28,20},{20,12},{12,4},{4,0},{1,9},{9... | collective-permute-start | bytes 3538952 | tf_op jit(solution)/shard_map/ppermute | solution.py:230
  1014.0 92.0 %collective-permute-start.39 = (bf16[3,8,16,1536]{3,2,1,0:T(8,128)(2,1)}, bf16[3,8,16,1536]{3,2,1,0:T(8,128)(2,1)}, u32[]{:S(2)}, u32[]{:S(2)}) collective-permute-start(bf16[3,8,16,1536]{3,2,1,0:T(8,128)(2,1)} %get-tuple-element.177), channel_id=1, source_target_pairs={{0,8},{8,16},{16,24},{24,28},{28,20},{20,12},{12,4},{4,0},{1,9},{9... | collective-permute-start | bytes 3538952 | tf_op jit(solution)/shard_map/ppermute | solution.py:230
  1015.5 92.9 %collective-permute-start.38 = (bf16[3,8,16,1536]{3,2,1,0:T(8,128)(2,1)}, bf16[3,8,16,1536]{3,2,1,0:T(8,128)(2,1)}, u32[]{:S(2)}, u32[]{:S(2)}) collective-permute-start(bf16[3,8,16,1536]{3,2,1,0:T(8,128)(2,1)} %get-tuple-element.176), channel_id=1, source_target_pairs={{0,4},{8,0},{16,8},{24,16},{28,24},{20,28},{12,20},{4,12},{1,5},{9... | collective-permute-start | bytes 3538952 | tf_op jit(solution)/shard_map/ppermute | solution.py:230
  1022.4 380.1 %reduce-scatter.9.cloned.1.call-start = ((), (), s32[]{:S(2)}) async-start(), calls=%async_computation.10 | async-start | bytes 4595712
  1040.6 74.5 %collective-permute-start.41 = (bf16[3,8,16,1536]{3,2,1,0:T(8,128)(2,1)S(1)}, bf16[3,8,16,1536]{3,2,1,0:T(8,128)(2,1)S(1)}, u32[]{:S(2)}, u32[]{:S(2)}) collective-permute-start(bf16[3,8,16,1536]{3,2,1,0:T(8,128)(2,1)S(1)} %copy-done.83), channel_id=1, source_target_pairs={{0,4},{8,0},{16,8},{24,16},{28,24},{20,28},{12,20},{4,12},{1,5},{9... | collective-permute-start | bytes 3538952 | tf_op jit(solution)/shard_map/ppermute | solution.py:230
  1045.5 85.6 %collective-permute-start.40 = (bf16[3,8,16,1536]{3,2,1,0:T(8,128)(2,1)S(1)}, bf16[3,8,16,1536]{3,2,1,0:T(8,128)(2,1)S(1)}, u32[]{:S(2)}, u32[]{:S(2)}) collective-permute-start(bf16[3,8,16,1536]{3,2,1,0:T(8,128)(2,1)S(1)} %copy-done.82), channel_id=1, source_target_pairs={{0,8},{8,16},{16,24},{24,28},{28,20},{20,12},{12,4},{4,0},{1,9},{9... | collective-permute-start | bytes 3538952 | tf_op jit(solution)/shard_map/ppermute | solution.py:230
  1073.3 62.6 %collective-permute-start.33 = (bf16[3,8,16,1536]{3,2,1,0:T(8,128)(2,1)S(1)}, bf16[3,8,16,1536]{3,2,1,0:T(8,128)(2,1)S(1)}, u32[]{:S(2)}, u32[]{:S(2)}) collective-permute-start(bf16[3,8,16,1536]{3,2,1,0:T(8,128)(2,1)S(1)} %copy-done.92), channel_id=1, source_target_pairs={{0,4},{8,0},{16,8},{24,16},{28,24},{20,28},{12,20},{4,12},{1,5},{9... | collective-permute-start | bytes 3538952 | tf_op jit(solution)/shard_map/ppermute | solution.py:230
  1106.0 47.8 %collective-permute-start.35 = (bf16[3,8,16,1536]{3,2,1,0:T(8,128)(2,1)S(1)}, bf16[3,8,16,1536]{3,2,1,0:T(8,128)(2,1)S(1)}, u32[]{:S(2)}, u32[]{:S(2)}) collective-permute-start(bf16[3,8,16,1536]{3,2,1,0:T(8,128)(2,1)S(1)} %copy-done.94), channel_id=1, source_target_pairs={{0,8},{8,16},{16,24},{24,28},{28,20},{20,12},{12,4},{4,0},{1,9},{9... | collective-permute-start | bytes 3538952 | tf_op jit(solution)/shard_map/ppermute | solution.py:230
  1175.9 56.5 %collective-permute-start.30 = (bf16[1024,1536]{1,0:T(8,128)(2,1)}, bf16[1024,1536]{1,0:T(8,128)(2,1)}, u32[]{:S(2)}, u32[]{:S(2)}) collective-permute-start(bf16[1024,1536]{1,0:T(8,128)(2,1)} %slice.695), channel_id=1, source_target_pairs={{0,2},{2,0},{1,3},{3,1},{4,6},{6,4},{5,7},{7,5},{8,10},{10,8},{9,1... | collective-permute-start | bytes 9437192 | tf_op jit(solution)/shard_map/ppermute | solution.py:153
  1213.1 112.9 %collective-permute-start.46 = (bf16[3,8,16,1536]{3,2,1,0:T(8,128)(2,1)}, bf16[3,8,16,1536]{3,2,1,0:T(8,128)(2,1)}, u32[]{:S(2)}, u32[]{:S(2)}) collective-permute-start(bf16[3,8,16,1536]{3,2,1,0:T(8,128)(2,1)} %add_convert_fusion.9), channel_id=1, source_target_pairs={{0,8},{8,16},{16,24},{24,28},{28,20},{20,12},{12,4},{4,0},{1,9},{9... | collective-permute-start | bytes 3538952 | tf_op jit(solution)/shard_map/ppermute | solution.py:230
  1214.8 140.9 %collective-permute-start.49 = (bf16[3,8,16,1536]{3,2,1,0:T(8,128)(2,1)}, bf16[3,8,16,1536]{3,2,1,0:T(8,128)(2,1)}, u32[]{:S(2)}, u32[]{:S(2)}) collective-permute-start(bf16[3,8,16,1536]{3,2,1,0:T(8,128)(2,1)} %get-tuple-element.201), channel_id=1, source_target_pairs={{0,8},{8,16},{16,24},{24,28},{28,20},{20,12},{12,4},{4,0},{1,9},{9... | collective-permute-start | bytes 3538952 | tf_op jit(solution)/shard_map/ppermute | solution.py:230
  1216.5 103.7 %collective-permute-start.47 = (bf16[3,8,16,1536]{3,2,1,0:T(8,128)(2,1)}, bf16[3,8,16,1536]{3,2,1,0:T(8,128)(2,1)}, u32[]{:S(2)}, u32[]{:S(2)}) collective-permute-start(bf16[3,8,16,1536]{3,2,1,0:T(8,128)(2,1)} %get-tuple-element.200), channel_id=1, source_target_pairs={{0,4},{8,0},{16,8},{24,16},{28,24},{20,28},{12,20},{4,12},{1,5},{9... | collective-permute-start | bytes 3538952 | tf_op jit(solution)/shard_map/ppermute | solution.py:230
  1216.8 99.4 %collective-permute-start.50 = (bf16[3,8,16,1536]{3,2,1,0:T(8,128)(2,1)}, bf16[3,8,16,1536]{3,2,1,0:T(8,128)(2,1)}, u32[]{:S(2)}, u32[]{:S(2)}) collective-permute-start(bf16[3,8,16,1536]{3,2,1,0:T(8,128)(2,1)} %get-tuple-element.202), channel_id=1, source_target_pairs={{0,8},{8,16},{16,24},{24,28},{28,20},{20,12},{12,4},{4,0},{1,9},{9... | collective-permute-start | bytes 3538952 | tf_op jit(solution)/shard_map/ppermute | solution.py:230
  1232.4 100.5 %collective-permute-start.53 = (bf16[3,8,16,1536]{3,2,1,0:T(8,128)(2,1)}, bf16[3,8,16,1536]{3,2,1,0:T(8,128)(2,1)}, u32[]{:S(2)}, u32[]{:S(2)}) collective-permute-start(bf16[3,8,16,1536]{3,2,1,0:T(8,128)(2,1)} %get-tuple-element.203), channel_id=1, source_target_pairs={{0,4},{8,0},{16,8},{24,16},{28,24},{20,28},{12,20},{4,12},{1,5},{9... | collective-permute-start | bytes 3538952 | tf_op jit(solution)/shard_map/ppermute | solution.py:230
  (195 other events, 3256.3 us)
Sparse Core Ops, SparseCore 0:
  10.8 53.7 all-gather.7
  67.0 41.9 all-gather.9
  110.5 97.6 all-gather.11
  209.7 98.8 all-gather.13
  310.0 98.8 all-gather.15
  410.3 98.8 all-gather.17
  510.8 98.8 all-gather.19
  1022.6 79.1 reduce-scatter.6
  1218.6 95.9 reduce-scatter.8
where the time goes:
time: 1420 us
  waiting for transfers between devices  503 us (35%)
  Pallas kernels  398 us (28%)
  other arithmetic  181 us (13%)
  local copies, waits for them, and re-layouts  126 us (9%)
  matrix products  112 us (8%)
  starting transfers between devices  64.7 us (5%)
  between operations  32 us (2%)
    pallas_call x5, Pallas kernels, expert_call(): pl.pallas_call(functools.partial(expert_kernel, first), grid_spec=pltpu.P...  398 us
    ppermute x35, waiting for transfers between devices, send(): return lax.ppermute(block, 'chip', pairs)  322 us
    ppermute x20, waiting for transfers between devices, swap(): return lax.ppermute(values, axis, [(0, 1), (1, 0)])  107 us
    convert_element_type x15, other arithmetic, add(): (block.astype(jnp.float32) + own.astype(jnp.float32)).astype(jnp.bfloat16)  65.3 us
    unnamed x347, local copies, waits for them, and re-layouts  62.4 us
    all_gather x5, waiting for transfers between devices, body(): gathered.append(lax.all_gather(part, ('chip', 'core'), axis=2, tiled=True))  60.7 us
    ppermute x35, starting transfers between devices, send(): return lax.ppermute(block, 'chip', pairs)  44.7 us
  transfers between devices with their start and end apart: 64, of which 30 were waited for; matrix products, arithmetic and copies ran while one was open for 22% of the time, Pallas kernels for 23%

commit v1 on v0

--- a/solution.py
+++ b/solution.py
@@ -20,10 +20,10 @@
     (),
     (),
     ((0, 1), (1, 1), (2, 1)),
-    ((0, 1), (1, 1), (2, 1), (3, 1)),
     ((0, 1), (1, 1), (2, 1), (3, 1), (4, 1)),
-    ((0, 1), (1, 1)),
-    ((2, 1), (3, 2), (4, 3)),
+    ((0, 1), (1, 1), (2, 1), (3, 1), (4, 1)),
+    ((0, 1), (1, 1), (3, 1)),
+    ((2, 1), (3, 1), (4, 2)),
 )
 BLOCK = 256
 RING = (0, 2, 4, 6, 7, 5, 3, 1)
@@ -216,14 +216,13 @@
     def __init__(self, grads, flip, starts):
         self.grads, self.step, self.hop_number = grads, -1 if flip else 1, 0
         self.count = len(RING)
-        self.rows = grads.shape[2] // self.count
         self.starts = starts
         far = self.count // 2
         self.state = (self.own(self.step * far), self.own(-self.step * (far - 1)))
 
     def own(self, ahead):
         start = self.starts[ahead % self.count]
-        return lax.dynamic_slice_in_dim(self.grads, start, self.rows, 2)
+        return lax.dynamic_index_in_dim(self.grads, start, 0, keepdims=False)
 
     def send(self, block, way):
         pairs = [(RING[i], RING[(i + way) % self.count]) for i in range(self.count)]
@@ -258,9 +257,7 @@
 
 class Whole:
     def __init__(self, grads):
-        self.state = lax.psum_scatter(
-            grads, "chip", scatter_dimension=2, tiled=True
-        )
+        self.state = lax.psum_scatter(grads, "chip", scatter_dimension=0, tiled=True)[0]
 
     def hop(self):
         pass
@@ -269,11 +266,11 @@
         return self.state.astype(jnp.float32)
 
 
-def ring_starts(rows):
+def ring_chips():
     count = len(RING)
     if lax.axis_size("chip") != count:
         return None
-    table = [[RING[(RING.index(c) + a) % count] * rows for a in range(count)] for c in range(count)]
+    table = [[RING[(RING.index(c) + a) % count] for a in range(count)] for c in range(count)]
     mine = jnp.asarray(table, jnp.int32)[lax.axis_index("chip")]
     return [mine[a] for a in range(count)]
 
@@ -373,7 +370,10 @@
         return carry
 
     lax.fori_loop(0, TILES, one_tile, 0)
-    grads_ref[...] = sums[...].astype(jnp.bfloat16).reshape(grads_ref.shape)
+    chips, _, _, shard, _ = grads_ref.shape
+    grads = sums[...].astype(jnp.bfloat16).reshape(3, 2, chips, shard, width)
+    for chip in range(chips):
+        grads_ref[chip] = grads[:, :, chip]
 
     @pl.when(step == steps - 1)
     def _():
@@ -411,7 +411,7 @@
                 anywhere,
                 anywhere,
                 by_pair,
-                pl.BlockSpec((3, 2, chips * shard, width), lambda i, core: (0, i, 0, 0)),
+                pl.BlockSpec((chips, 3, 2, shard, width), lambda i, core: (0, 0, i, 0, 0)),
             ],
             scratch_shapes=[
                 pltpu.VMEM((count, width), jnp.float32),
@@ -425,7 +425,7 @@
             total,
             total,
             jax.ShapeDtypeStruct(gates.shape, jnp.float32),
-            jax.ShapeDtypeStruct((3, each, chips * shard, width), jnp.bfloat16),
+            jax.ShapeDtypeStruct((chips, 3, each, shard, width), jnp.bfloat16),
         ],
         input_output_aliases={} if first else {5: 0, 6: 1},
         compiler_params=pltpu.CompilerParams(vmem_limit_bytes=67043328),
@@ -491,21 +491,20 @@
     inputs_f = inputs.astype(jnp.float32)
     q_cols, k_cols = w_query.shape[1], w_key.shape[1]
     proj_cols = q_cols + 2 * k_cols
-    filler = jnp.zeros((w_query.shape[0], 127), jnp.bfloat16)
-    packed = jnp.concatenate([w_query, w_key, w_value, gain_attn[:, None], filler], axis=1)
+    filler = jnp.zeros((w_query.shape[0], 126 - E), jnp.bfloat16)
+    packed = jnp.concatenate(
+        [w_query, w_key, w_value, w_out.T, w_router, gain_attn[:, None], gain_moe[:, None], filler],
+        axis=1,
+    )
     packed = lax.all_gather(packed, ("chip", "core"), axis=0, tiled=True)
-    proj_w, gain_one_f = packed[:, :proj_cols], packed[:, proj_cols].astype(jnp.float32)
+    proj_w, out_wt, small = jnp.split(packed, [proj_cols, proj_cols + q_cols], axis=1)
     query_w, key_w, value_w = jnp.split(proj_w, [q_cols, q_cols + k_cols], axis=1)
-    packed = jnp.concatenate(
-        [w_out.T, w_router, gain_moe[:, None], filler[:, : 127 - E]], axis=1
-    )
-    packed, _ = lax.optimization_barrier((packed, proj_w))
-    packed = lax.all_gather(packed, ("chip", "core"), axis=0, tiled=True)
-    out_wt, router_w = packed[:, :q_cols], packed[:, q_cols : q_cols + E]
-    gain_two_f = packed[:, q_cols + E].astype(jnp.float32)
+    router_w = small[:, :E]
+    gain_one_f = small[:, E].astype(jnp.float32)
+    gain_two_f = small[:, E + 1].astype(jnp.float32)
 
     shard = w_gate.shape[1] // D
-    starts = ring_starts(shard)
+    starts = ring_chips()
     groups = GROUPS
     each = E // groups
     stacked = [w.reshape(E, shard, D) for w in (w_gate, w_up, w_down)]
@@ -585,6 +584,7 @@
                 token_rows_g, cot_rows_g, group_gates, gate_w, up_w, down_w
             )
             mixture, rows_grad = mixture + mix, rows_grad + rows
+            grads = jnp.moveaxis(grads.reshape(3, each, -1, shard, D), 2, 0)
         gate_grads.append(gate_grad)
     run_hops(expert_sums, groups - 1)
     mixture, rows_grad, grads = tie(
@@ -611,9 +611,8 @@
         preferred_element_type=jnp.float32,
     )
     half_rows = seq_len
-    mine = rows_grad[:half_rows] + swap(
-        rows_grad[half_rows:].astype(jnp.bfloat16), "core"
-    ).astype(jnp.float32)
+    theirs = rows_grad[half_rows:].astype(jnp.bfloat16)
+    mine = rows_grad[:half_rows] + swap(theirs, "core").astype(jnp.float32)
     mid_parts, gain_two_grad = [], 0.0
     for c in range(chunks):
         part = slice(c * piece, (c + 1) * piece)
@@ -640,7 +639,10 @@
         mid_all = gather_ordered(mid_grad.astype(jnp.bfloat16))
     run_hops(expert_sums, groups)
     mid_all, mixture = tie((mid_all, mixture), expert_sums)
-    outputs = (hidden_mid + scatter_rows(mixture)).astype(jnp.bfloat16)
+    mixed = swap(mixture[seq_len:].astype(jnp.bfloat16), "core")
+    mixed = (mixture[:seq_len] + mixed.astype(jnp.float32)).astype(jnp.bfloat16)
+    mixed = scatter_tensor(mixed, False)
+    outputs = (hidden_mid + mixed).astype(jnp.bfloat16)
     out_wt_grad = lax.dot_general(
         mid_all, attn_out, contract_first, preferred_element_type=jnp.float32
     )
@@ -670,12 +672,10 @@
     proj_w_grad = lax.dot_general(
         normed_all, proj_pg, contract_first, preferred_element_type=jnp.float32
     )
-    normed_one_grad = scatter_tensor(
-        lax.dot_general(
-            proj_pg, proj_w, contract_last, preferred_element_type=jnp.float32
-        ).astype(jnp.bfloat16),
-        True,
-    )
+    summed = lax.dot_general(
+        proj_pg, proj_w, contract_last, preferred_element_type=jnp.float32
+    ).astype(jnp.bfloat16)
+    normed_one_grad = scatter_tensor(summed, True)
     input_part, gain_one_grad = norm_backward(inputs_f, scale_one, gain_one_f, normed_one_grad)
     input_grad = mid_grad + input_part
     late = jnp.concatenate(
@@ -696,8 +696,8 @@
         shared = shared + swap(shared, "tensor")
     else:
         shared = lax.psum(shared, "tensor")
-    expert_grads = jnp.concatenate([each.result() for each in expert_sums], axis=1)
-    expert_grads = expert_grads.reshape(3, E, shard * D)
+    pieces = [each_sum.result().reshape(3, each, shard * D) for each_sum in expert_sums]
+    expert_grads = [jnp.concatenate([piece[k] for piece in pieces], axis=0) for k in range(3)]
     return (
         outputs,
         input_grad,

time: 1420 us -> 1360 us (0.958)
  waiting for transfers between devices: 503 us -> 442 us
    all_gather x5, waiting for transfers between devices: 60.7 us -> 37.4 us  [body(): gathered.append(lax.all_gather(part, ('chip', 'core'), axis=2, tiled=True))]
    ppermute x35, waiting for transfers between devices: 322 us -> 302 us  [send(): return lax.ppermute(block, 'chip', pairs)]
    unnamed x15 -> x11, other arithmetic: 20.1 us -> 2.87 us
    dynamic_slice x6 -> x1, local copies, waits for them, and re-layouts: 16.9 us -> 0.7 us  [ring_chips(): mine = jnp.asarray(table, jnp.int32)[lax.axis_index('chip')]]
    unnamed x347 -> x374, local copies, waits for them, and re-layouts: 62.4 us -> 71.7 us
  transfers between devices with their start and end apart: 64 -> 63, of which waited for: 30 -> 32; matrix products, arithmetic and copies ran while one was open for 22% -> 22% of each run, Pallas kernels for 23% -> 24%
where the time goes in v1:
time: 1360 us; the launch traced here: 1350 us
  waiting for transfers between devices  442 us (32%)
  Pallas kernels  400 us (29%)
  other arithmetic  168 us (12%)
  local copies, waits for them, and re-layouts  126 us (9%)
  matrix products  114 us (8%)
  starting transfers between devices  65.8 us (5%)
  between operations  32.2 us (2%)
    pallas_call x5, Pallas kernels, expert_call(): pl.pallas_call(functools.partial(expert_kernel, first), grid_spec=pltpu.P...  400 us
    ppermute x35, waiting for transfers between devices, send(): return lax.ppermute(block, 'chip', pairs)  302 us
    ppermute x20, waiting for transfers between devices, swap(): return lax.ppermute(values, axis, [(0, 1), (1, 0)])  95.9 us
    unnamed x374, local copies, waits for them, and re-layouts  71.7 us
    convert_element_type x15, other arithmetic, add(): (block.astype(jnp.float32) + own.astype(jnp.float32)).astype(jnp.bfloat16)  56.1 us
    ppermute x35, starting transfers between devices, send(): return lax.ppermute(block, 'chip', pairs)  44 us
    all_gather x5, waiting for transfers between devices, body(): gathered.append(lax.all_gather(part, ('chip', 'core'), axis=2, tiled=True))  37.4 us
  transfers between devices with their start and end apart: 63, of which 32 were waited for; matrix products, arithmetic and copies ran while one was open for 22% of the time, Pallas kernels for 24%

profile of v1, /device:TPU:0, one launch (start us, length us, event | category | flops | bytes accessed | tf_op | source)
XLA Modules:
  0.0 1348.8 jit_solution(14626305492668548018)
XLA Ops:
  31.4 31.6 %collective-permute-done = bf16[512,1536]{1,0:T(8,128)(2,1)} collective-permute-done((bf16[512,1536]{1,0:T(8,128)(2,1)S(1)}, bf16[512,1536]{1,0:T(8,128)(2,1)}, u32[]{:S(2)}, u32[]{:S(2)}) %collective-permute-start) | collective-permute-done | bytes 1572896 | tf_op jit(solution)/shard_map/ppermute | solution.py:153
  127.6 13.3 collective-permute-done.2
  167.0 14.1 %collective-permute-done.4 = bf16[256,1536]{1,0:T(8,128)(2,1)} collective-permute-done((bf16[256,1536]{1,0:T(8,128)(2,1)}, bf16[256,1536]{1,0:T(8,128)(2,1)}, u32[]{:S(2)}, u32[]{:S(2)}) %collective-permute-start.4) | collective-permute-done | bytes 786464 | tf_op jit(solution)/shard_map/ppermute | solution.py:153
  214.9 80.2 %experts.5 = (f32[2048,1536]{1,0:T(8,128)}, f32[2048,1536]{1,0:T(8,128)}, f32[4,2,2048]{2,1,0:T(2,128)}, bf16[8,3,8,16,1536]{4,3,2,1,0:T(8,128)(2,1)}) custom-call(s32[1]{0:T(128)} %bitcast.40.core_ref, bf16[2048,1536]{1,0:T(8,128)(2,1)} %copy-done.17, bf16[2048,1536]{1,0:T(8,128)(2,1)} %copy-done.98, f32[4,2,2048]{2,1,0:T(2,128)} %reshape.481.gates_ref, ...), custom_call_target="tpu_custom_call" | custom-call | flops 57982058496 | bytes 69206016 | tf_op jit(solution)/shard_map/experts/pallas_call | solution.py:396
  296.6 80.2 %experts.6 = (f32[2048,1536]{1,0:T(8,128)}, f32[2048,1536]{1,0:T(8,128)}, f32[4,2,2048]{2,1,0:T(2,128)}, bf16[8,3,8,16,1536]{4,3,2,1,0:T(8,128)(2,1)}) custom-call(s32[1]{0:T(128)} %bitcast.40.core_ref, bf16[2048,1536]{1,0:T(8,128)(2,1)} %copy-done.17, bf16[2048,1536]{1,0:T(8,128)(2,1)} %copy-done.98, ...), custom_call_target="tpu_custom_call", output_to_operand_aliasing={{0}: (5, {}), {1}: (6, {})} | custom-call | flops 57982058496 | bytes 69206016 | tf_op jit(solution)/shard_map/experts/pallas_call | solution.py:396
  378.4 79.7 %experts.7 = (f32[2048,1536]{1,0:T(8,128)}, f32[2048,1536]{1,0:T(8,128)}, f32[4,2,2048]{2,1,0:T(2,128)}, bf16[8,3,8,16,1536]{4,3,2,1,0:T(8,128)(2,1)}) custom-call(s32[1]{0:T(128)} %bitcast.40.core_ref, bf16[2048,1536]{1,0:T(8,128)(2,1)} %copy-done.17, bf16[2048,1536]{1,0:T(8,128)(2,1)} %copy-done.98, ...), custom_call_target="tpu_custom_call", output_to_operand_aliasing={{0}: (5, {}), {1}: (6, {})} | custom-call | flops 57982058496 | bytes 69206016 | tf_op jit(solution)/shard_map/experts/pallas_call | solution.py:396
  459.6 18.9 %all-gather.15.cloned.1.call-done = bf16[3,8,256,1536]{3,2,1,0:T(8,128)(2,1)} async-done(((bf16[3,8,16,1536]{3,2,1,0:T(8,128)(2,1)}), bf16[3,8,256,1536]{3,2,1,0:T(8,128)(2,1)}) %all-gather.15.cloned.1.call-update) | async-done | bytes 18874384 | tf_op jit(solution)/shard_map/all_gather | solution.py:514
  480.0 80.3 %experts.8 = (f32[2048,1536]{1,0:T(8,128)}, f32[2048,1536]{1,0:T(8,128)}, f32[4,2,2048]{2,1,0:T(2,128)}, bf16[8,3,8,16,1536]{4,3,2,1,0:T(8,128)(2,1)}) custom-call(s32[1]{0:T(128)} %bitcast.40.core_ref, bf16[2048,1536]{1,0:T(8,128)(2,1)} %copy-done.17, bf16[2048,1536]{1,0:T(8,128)(2,1)} %copy-done.98, ...), custom_call_target="tpu_custom_call", output_to_operand_aliasing={{0}: (5, {}), {1}: (6, {})} | custom-call | flops 57982058496 | bytes 69206016 | tf_op jit(solution)/shard_map/experts/pallas_call | solution.py:396
  560.3 18.5 %all-gather.17.cloned.1.call-done = bf16[3,8,256,1536]{3,2,1,0:T(8,128)(2,1)} async-done(((bf16[3,8,16,1536]{3,2,1,0:T(8,128)(2,1)}), bf16[3,8,256,1536]{3,2,1,0:T(8,128)(2,1)}) %all-gather.17.cloned.1.call-update) | async-done | bytes 18874384 | tf_op jit(solution)/shard_map/all_gather | solution.py:514
  578.8 79.3 %experts.9 = (f32[2048,1536]{1,0:T(8,128)}, f32[2048,1536]{1,0:T(8,128)}, f32[4,2,2048]{2,1,0:T(2,128)}, bf16[8,3,8,16,1536]{4,3,2,1,0:T(8,128)(2,1)}) custom-call(s32[1]{0:T(128)} %bitcast.40.core_ref, bf16[2048,1536]{1,0:T(8,128)(2,1)} %copy-done.17, bf16[2048,1536]{1,0:T(8,128)(2,1)} %copy-done.98, ...), custom_call_target="tpu_custom_call", output_to_operand_aliasing={{0}: (5, {}), {1}: (6, {})} | custom-call | flops 57982058496 | bytes 69206016 | tf_op jit(solution)/shard_map/experts/pallas_call | solution.py:396
  677.4 14.2 %collective-permute-done.10 = bf16[3,8,16,1536]{3,2,1,0:T(8,128)(2,1)} collective-permute-done((bf16[3,8,16,1536]{3,2,1,0:T(8,128)(2,1)}, bf16[3,8,16,1536]{3,2,1,0:T(8,128)(2,1)}, u32[]{:S(2)}, u32[]{:S(2)}) %collective-permute-start.10) | collective-permute-done | bytes 1179680 | tf_op jit(solution)/shard_map/ppermute | solution.py:229
  696.4 20.6 %collective-permute-done.14 = bf16[3,8,16,1536]{3,2,1,0:T(8,128)(2,1)} collective-permute-done((bf16[3,8,16,1536]{3,2,1,0:T(8,128)(2,1)}, bf16[3,8,16,1536]{3,2,1,0:T(8,128)(2,1)}, u32[]{:S(2)}, u32[]{:S(2)}) %collective-permute-start.14) | collective-permute-done | bytes 1179680 | tf_op jit(solution)/shard_map/ppermute | solution.py:229
  716.9 25.3 %collective-permute-done.13 = bf16[3,8,16,1536]{3,2,1,0:T(8,128)(2,1)} collective-permute-done((bf16[3,8,16,1536]{3,2,1,0:T(8,128)(2,1)}, bf16[3,8,16,1536]{3,2,1,0:T(8,128)(2,1)}, u32[]{:S(2)}, u32[]{:S(2)}) %collective-permute-start.13) | collective-permute-done | bytes 1179680 | tf_op jit(solution)/shard_map/ppermute | solution.py:229
  771.4 14.9 %collective-permute-done.29 = bf16[3,8,16,1536]{3,2,1,0:T(8,128)(2,1)S(1)} collective-permute-done((bf16[3,8,16,1536]{3,2,1,0:T(8,128)(2,1)S(1)}, bf16[3,8,16,1536]{3,2,1,0:T(8,128)(2,1)S(1)}, u32[]{:S(2)}, u32[]{:S(2)}) %collective-permute-start.29) | collective-permute-done | bytes 1179680 | tf_op jit(solution)/shard_map/ppermute | solution.py:229
  790.6 21.7 %collective-permute-done.23 = bf16[3,8,16,1536]{3,2,1,0:T(8,128)(2,1)S(1)} collective-permute-done((bf16[3,8,16,1536]{3,2,1,0:T(8,128)(2,1)S(1)}, bf16[3,8,16,1536]{3,2,1,0:T(8,128)(2,1)S(1)}, u32[]{:S(2)}, u32[]{:S(2)}) %collective-permute-start.23) | collective-permute-done | bytes 1179680 | tf_op jit(solution)/shard_map/ppermute | solution.py:229
  829.5 8.3 collective-permute-done.27
  839.2 23.1 %collective-permute-done.26 = bf16[3,8,16,1536]{3,2,1,0:T(8,128)(2,1)} collective-permute-done((bf16[3,8,16,1536]{3,2,1,0:T(8,128)(2,1)}, bf16[3,8,16,1536]{3,2,1,0:T(8,128)(2,1)}, u32[]{:S(2)}, u32[]{:S(2)}) %collective-permute-start.26) | collective-permute-done | bytes 1179680 | tf_op jit(solution)/shard_map/ppermute | solution.py:229
  870.5 16.2 %collective-permute-done.30 = bf16[3,8,16,1536]{3,2,1,0:T(8,128)(2,1)} collective-permute-done((bf16[3,8,16,1536]{3,2,1,0:T(8,128)(2,1)}, bf16[3,8,16,1536]{3,2,1,0:T(8,128)(2,1)}, u32[]{:S(2)}, u32[]{:S(2)}) %collective-permute-start.30) | collective-permute-done | bytes 1179680 | tf_op jit(solution)/shard_map/ppermute | solution.py:229
  908.4 11.1 collective-permute-done.20
  919.6 15.0 %collective-permute-done.21 = bf16[256,1536]{1,0:T(8,128)(2,1)S(1)} collective-permute-done((bf16[256,1536]{1,0:T(8,128)(2,1)S(1)}, bf16[256,1536]{1,0:T(8,128)(2,1)S(1)}, u32[]{:S(2)}, u32[]{:S(2)}) %collective-permute-start.21) | collective-permute-done | bytes 786464 | tf_op jit(solution)/shard_map/ppermute | solution.py:153
  946.7 10.6 fusion.9
  964.1 7.4 fusion.16
  1031.3 9.0 collective-permute-done.34
  1048.9 16.7 %collective-permute-done.38 = bf16[3,8,16,1536]{3,2,1,0:T(8,128)(2,1)} collective-permute-done((bf16[3,8,16,1536]{3,2,1,0:T(8,128)(2,1)}, bf16[3,8,16,1536]{3,2,1,0:T(8,128)(2,1)}, u32[]{:S(2)}, u32[]{:S(2)}) %collective-permute-start.38) | collective-permute-done | bytes 1179680 | tf_op jit(solution)/shard_map/ppermute | solution.py:229
  1070.1 20.8 %collective-permute-done.41 = bf16[3,8,16,1536]{3,2,1,0:T(8,128)(2,1)} collective-permute-done((bf16[3,8,16,1536]{3,2,1,0:T(8,128)(2,1)}, bf16[3,8,16,1536]{3,2,1,0:T(8,128)(2,1)}, u32[]{:S(2)}, u32[]{:S(2)}) %collective-permute-start.41) | collective-permute-done | bytes 1179680 | tf_op jit(solution)/shard_map/ppermute | solution.py:229
  1097.7 18.4 %collective-permute-done.42 = bf16[3,8,16,1536]{3,2,1,0:T(8,128)(2,1)S(1)} collective-permute-done((bf16[3,8,16,1536]{3,2,1,0:T(8,128)(2,1)S(1)}, bf16[3,8,16,1536]{3,2,1,0:T(8,128)(2,1)S(1)}, u32[]{:S(2)}, u32[]{:S(2)}) %collective-permute-start.42) | collective-permute-done | bytes 1179680 | tf_op jit(solution)/shard_map/ppermute | solution.py:229
  1120.1 18.6 %collective-permute-done.37 = bf16[3,8,16,1536]{3,2,1,0:T(8,128)(2,1)S(1)} collective-permute-done((bf16[3,8,16,1536]{3,2,1,0:T(8,128)(2,1)S(1)}, bf16[3,8,16,1536]{3,2,1,0:T(8,128)(2,1)S(1)}, u32[]{:S(2)}, u32[]{:S(2)}) %collective-permute-start.37) | collective-permute-done | bytes 1179680 | tf_op jit(solution)/shard_map/ppermute | solution.py:229
  1174.2 7.4 collective-permute-done.44
  1187.0 11.8 collective-permute-done.46
  1198.8 17.6 %collective-permute-done.48 = bf16[3,8,16,1536]{3,2,1,0:T(8,128)(2,1)S(1)} collective-permute-done((bf16[3,8,16,1536]{3,2,1,0:T(8,128)(2,1)S(1)}, bf16[3,8,16,1536]{3,2,1,0:T(8,128)(2,1)S(1)}, u32[]{:S(2)}, u32[]{:S(2)}) %collective-permute-start.48) | collective-permute-done | bytes 1179680 | tf_op jit(solution)/shard_map/ppermute | solution.py:229
  1261.3 20.8 %collective-permute-done.50 = bf16[3,8,16,1536]{3,2,1,0:T(8,128)(2,1)} collective-permute-done((bf16[3,8,16,1536]{3,2,1,0:T(8,128)(2,1)}, bf16[3,8,16,1536]{3,2,1,0:T(8,128)(2,1)}, u32[]{:S(2)}, u32[]{:S(2)}) %collective-permute-start.50) | collective-permute-done | bytes 1179680 | tf_op jit(solution)/shard_map/ppermute | solution.py:229
  1310.4 16.8 %collective-permute-done.53 = bf16[3,8,16,1536]{3,2,1,0:T(8,128)(2,1)} collective-permute-done((bf16[3,8,16,1536]{3,2,1,0:T(8,128)(2,1)}, bf16[3,8,16,1536]{3,2,1,0:T(8,128)(2,1)}, u32[]{:S(2)}, u32[]{:S(2)}) %collective-permute-start.53) | collective-permute-done | bytes 1179680 | tf_op jit(solution)/shard_map/ppermute | solution.py:229
  (693 shorter events, 474.1 us)
Async XLA Ops:
  7.2 71.0 %all-gather.7.cloned.1.call-start = ((), (), s32[]{:S(2)}) async-start(), calls=%async_computation.2 | async-start | bytes 7102464 | tf_op jit(solution)/shard_map/all_gather | solution.py:499
  11.6 203.2 %all-gather.9.cloned.1.call-start = ((), (), s32[]{:S(2)}) async-start(), calls=%async_computation.3 | async-start | bytes 20054016 | tf_op jit(solution)/shard_map/all_gather | solution.py:514
  18.3 278.3 %all-gather.11.cloned.1.call-start = ((), (), s32[]{:S(2)}) async-start(), calls=%async_computation.4 | async-start | bytes 20054016 | tf_op jit(solution)/shard_map/all_gather | solution.py:514
  21.0 357.4 %all-gather.13.cloned.1.call-start = ((), (), s32[]{:S(2)}) async-start(), calls=%async_computation.5 | async-start | bytes 20054016 | tf_op jit(solution)/shard_map/all_gather | solution.py:514
  22.6 455.9 %all-gather.15.cloned.1.call-start = ((), (), s32[]{:S(2)}) async-start(), calls=%async_computation.6 | async-start | bytes 20054016 | tf_op jit(solution)/shard_map/all_gather | solution.py:514
  25.5 553.3 %all-gather.17.cloned.1.call-start = ((), (), s32[]{:S(2)}) async-start(), calls=%async_computation.7 | async-start | bytes 20054016 | tf_op jit(solution)/shard_map/all_gather | solution.py:514
  30.0 1273.9 %reduce-scatter.7.cloned.1.call-start = ((), (), s32[]{:S(2)}) async-start(), calls=%async_computation.8 | async-start | bytes 2924544
  69.0 54.1 %collective-permute-start.6 = (bf16[512,1536]{1,0:T(8,128)(2,1)}, bf16[512,1536]{1,0:T(8,128)(2,1)}, u32[]{:S(2)}, u32[]{:S(2)}) collective-permute-start(bf16[512,1536]{1,0:T(8,128)(2,1)} %param.26), channel_id=1, source_target_pairs={{0,1},{1,0},{2,3},{3,2},{4,5},{5,4},{6,7},{7,6},{8,9},{9,8},{10,11... | collective-permute-start | bytes 4718600 | tf_op jit(solution)/shard_map/ppermute | solution.py:153
  127.1 59.9 %collective-permute-start.7 = (bf16[1024,1536]{1,0:T(8,128)(2,1)}, bf16[1024,1536]{1,0:T(8,128)(2,1)}, u32[]{:S(2)}, u32[]{:S(2)}) collective-permute-start(bf16[1024,1536]{1,0:T(8,128)(2,1)} %pad_maximum_fusion.3), channel_id=1, source_target_pairs={{0,2},{2,0},{1,3},{3,1},{4,6},{6,4},{5,7},{7,5},{8,10},{10,8},{9,1... | collective-permute-start | bytes 9437192 | tf_op jit(solution)/shard_map/ppermute | solution.py:153
  666.3 80.9 %collective-permute-start.12 = (bf16[3,8,16,1536]{3,2,1,0:T(8,128)(2,1)S(1)}, bf16[3,8,16,1536]{3,2,1,0:T(8,128)(2,1)}, u32[]{:S(2)}, u32[]{:S(2)}) collective-permute-start(bf16[3,8,16,1536]{3,2,1,0:T(8,128)(2,1)S(1)} %get-tuple-element.302), channel_id=1, source_target_pairs={{0,8},{8,16},{16,24},{24,28},{28,20},{20,12},{12,4},{4,0},{1,9},{9... | collective-permute-start | bytes 3538952 | tf_op jit(solution)/shard_map/ppermute | solution.py:229
  671.7 70.6 %collective-permute-start.13 = (bf16[3,8,16,1536]{3,2,1,0:T(8,128)(2,1)}, bf16[3,8,16,1536]{3,2,1,0:T(8,128)(2,1)}, u32[]{:S(2)}, u32[]{:S(2)}) collective-permute-start(bf16[3,8,16,1536]{3,2,1,0:T(8,128)(2,1)} %get-tuple-element.299), channel_id=1, source_target_pairs={{0,8},{8,16},{16,24},{24,28},{28,20},{20,12},{12,4},{4,0},{1,9},{9... | collective-permute-start | bytes 3538952 | tf_op jit(solution)/shard_map/ppermute | solution.py:229
  691.6 55.5 %collective-permute-start.11 = (bf16[3,8,16,1536]{3,2,1,0:T(8,128)(2,1)S(1)}, bf16[3,8,16,1536]{3,2,1,0:T(8,128)(2,1)S(1)}, u32[]{:S(2)}, u32[]{:S(2)}) collective-permute-start(bf16[3,8,16,1536]{3,2,1,0:T(8,128)(2,1)S(1)} %get-tuple-element.303), channel_id=1, source_target_pairs={{0,4},{8,0},{16,8},{24,16},{28,24},{20,28},{12,20},{4,12},{1,5},{9... | collective-permute-start | bytes 3538952 | tf_op jit(solution)/shard_map/ppermute | solution.py:229
  755.0 63.3 %collective-permute-start.15 = (bf16[1024,1536]{1,0:T(8,128)(2,1)S(1)}, bf16[1024,1536]{1,0:T(8,128)(2,1)S(1)}, u32[]{:S(2)}, u32[]{:S(2)}) collective-permute-start(bf16[1024,1536]{1,0:T(8,128)(2,1)S(1)} %slice.762), channel_id=1, source_target_pairs={{0,2},{2,0},{1,3},{3,1},{4,6},{6,4},{5,7},{7,5},{8,10},{10,8},{9,1... | collective-permute-start | bytes 9437192 | tf_op jit(solution)/shard_map/ppermute | solution.py:153
  786.3 114.8 %collective-permute-start.25 = (bf16[3,8,16,1536]{3,2,1,0:T(8,128)(2,1)}, bf16[3,8,16,1536]{3,2,1,0:T(8,128)(2,1)}, u32[]{:S(2)}, u32[]{:S(2)}) collective-permute-start(bf16[3,8,16,1536]{3,2,1,0:T(8,128)(2,1)} %get-tuple-element.161), channel_id=1, source_target_pairs={{0,8},{8,16},{16,24},{24,28},{28,20},{20,12},{12,4},{4,0},{1,9},{9... | collective-permute-start | bytes 3538952 | tf_op jit(solution)/shard_map/ppermute | solution.py:229
  787.1 50.7 %collective-permute-start.27 = (bf16[3,8,16,1536]{3,2,1,0:T(8,128)(2,1)}, bf16[3,8,16,1536]{3,2,1,0:T(8,128)(2,1)}, u32[]{:S(2)}, u32[]{:S(2)}) collective-permute-start(bf16[3,8,16,1536]{3,2,1,0:T(8,128)(2,1)} %get-tuple-element.163), channel_id=1, source_target_pairs={{0,4},{8,0},{16,8},{24,16},{28,24},{20,28},{12,20},{4,12},{1,5},{9... | collective-permute-start | bytes 3538952 | tf_op jit(solution)/shard_map/ppermute | solution.py:229
  812.4 49.9 %collective-permute-start.26 = (bf16[3,8,16,1536]{3,2,1,0:T(8,128)(2,1)}, bf16[3,8,16,1536]{3,2,1,0:T(8,128)(2,1)}, u32[]{:S(2)}, u32[]{:S(2)}) collective-permute-start(bf16[3,8,16,1536]{3,2,1,0:T(8,128)(2,1)} %get-tuple-element.162), channel_id=1, source_target_pairs={{0,8},{8,16},{16,24},{24,28},{28,20},{20,12},{12,4},{4,0},{1,9},{9... | collective-permute-start | bytes 3538952 | tf_op jit(solution)/shard_map/ppermute | solution.py:229
  813.9 54.6 %collective-permute-start.31 = (bf16[3,8,16,1536]{3,2,1,0:T(8,128)(2,1)}, bf16[3,8,16,1536]{3,2,1,0:T(8,128)(2,1)}, u32[]{:S(2)}, u32[]{:S(2)}) collective-permute-start(bf16[3,8,16,1536]{3,2,1,0:T(8,128)(2,1)} %get-tuple-element.284), channel_id=1, source_target_pairs={{0,4},{8,0},{16,8},{24,16},{28,24},{20,28},{12,20},{4,12},{1,5},{9... | collective-permute-start | bytes 3538952 | tf_op jit(solution)/shard_map/ppermute | solution.py:229
  820.0 66.6 %collective-permute-start.30 = (bf16[3,8,16,1536]{3,2,1,0:T(8,128)(2,1)}, bf16[3,8,16,1536]{3,2,1,0:T(8,128)(2,1)}, u32[]{:S(2)}, u32[]{:S(2)}) collective-permute-start(bf16[3,8,16,1536]{3,2,1,0:T(8,128)(2,1)} %get-tuple-element.285), channel_id=1, source_target_pairs={{0,8},{8,16},{16,24},{24,28},{28,20},{20,12},{12,4},{4,0},{1,9},{9... | collective-permute-start | bytes 3538952 | tf_op jit(solution)/shard_map/ppermute | solution.py:229
  837.8 52.9 %collective-permute-start.19 = (bf16[256,1536]{1,0:T(8,128)(2,1)S(1)}, bf16[256,1536]{1,0:T(8,128)(2,1)S(1)}, u32[]{:S(2)}, u32[]{:S(2)}) collective-permute-start(bf16[256,1536]{1,0:T(8,128)(2,1)S(1)} %get-tuple-element.314), channel_id=1, source_target_pairs={{0,1},{1,0},{2,3},{3,2},{4,5},{5,4},{6,7},{7,6},{8,9},{9,8},{10,11... | collective-permute-start | bytes 2359304 | tf_op jit(solution)/shard_map/ppermute | solution.py:153
  1013.2 52.4 %collective-permute-start.38 = (bf16[3,8,16,1536]{3,2,1,0:T(8,128)(2,1)}, bf16[3,8,16,1536]{3,2,1,0:T(8,128)(2,1)}, u32[]{:S(2)}, u32[]{:S(2)}) collective-permute-start(bf16[3,8,16,1536]{3,2,1,0:T(8,128)(2,1)} %get-tuple-element.172), channel_id=1, source_target_pairs={{0,8},{8,16},{16,24},{24,28},{28,20},{20,12},{12,4},{4,0},{1,9},{9... | collective-permute-start | bytes 3538952 | tf_op jit(solution)/shard_map/ppermute | solution.py:229
  1014.0 76.9 %collective-permute-start.41 = (bf16[3,8,16,1536]{3,2,1,0:T(8,128)(2,1)}, bf16[3,8,16,1536]{3,2,1,0:T(8,128)(2,1)}, u32[]{:S(2)}, u32[]{:S(2)}) collective-permute-start(bf16[3,8,16,1536]{3,2,1,0:T(8,128)(2,1)} %get-tuple-element.175), channel_id=1, source_target_pairs={{0,8},{8,16},{16,24},{24,28},{28,20},{20,12},{12,4},{4,0},{1,9},{9... | collective-permute-start | bytes 3538952 | tf_op jit(solution)/shard_map/ppermute | solution.py:229
  1015.5 76.2 %collective-permute-start.40 = (bf16[3,8,16,1536]{3,2,1,0:T(8,128)(2,1)}, bf16[3,8,16,1536]{3,2,1,0:T(8,128)(2,1)}, u32[]{:S(2)}, u32[]{:S(2)}) collective-permute-start(bf16[3,8,16,1536]{3,2,1,0:T(8,128)(2,1)} %get-tuple-element.174), channel_id=1, source_target_pairs={{0,4},{8,0},{16,8},{24,16},{28,24},{20,28},{12,20},{4,12},{1,5},{9... | collective-permute-start | bytes 3538952 | tf_op jit(solution)/shard_map/ppermute | solution.py:229
  1040.3 57.2 %collective-permute-start.43 = (bf16[3,8,16,1536]{3,2,1,0:T(8,128)(2,1)S(1)}, bf16[3,8,16,1536]{3,2,1,0:T(8,128)(2,1)S(1)}, u32[]{:S(2)}, u32[]{:S(2)}) collective-permute-start(bf16[3,8,16,1536]{3,2,1,0:T(8,128)(2,1)S(1)} %copy-done.88), channel_id=1, source_target_pairs={{0,4},{8,0},{16,8},{24,16},{28,24},{20,28},{12,20},{4,12},{1,5},{9... | collective-permute-start | bytes 3538952 | tf_op jit(solution)/shard_map/ppermute | solution.py:229
  1044.9 71.2 %collective-permute-start.42 = (bf16[3,8,16,1536]{3,2,1,0:T(8,128)(2,1)S(1)}, bf16[3,8,16,1536]{3,2,1,0:T(8,128)(2,1)S(1)}, u32[]{:S(2)}, u32[]{:S(2)}) collective-permute-start(bf16[3,8,16,1536]{3,2,1,0:T(8,128)(2,1)S(1)} %copy-done.87), channel_id=1, source_target_pairs={{0,8},{8,16},{16,24},{24,28},{28,20},{20,12},{12,4},{4,0},{1,9},{9... | collective-permute-start | bytes 3538952 | tf_op jit(solution)/shard_map/ppermute | solution.py:229
  1065.6 54.5 %collective-permute-start.35 = (bf16[3,8,16,1536]{3,2,1,0:T(8,128)(2,1)S(1)}, bf16[3,8,16,1536]{3,2,1,0:T(8,128)(2,1)S(1)}, u32[]{:S(2)}, u32[]{:S(2)}) collective-permute-start(bf16[3,8,16,1536]{3,2,1,0:T(8,128)(2,1)S(1)} %copy-done.85), channel_id=1, source_target_pairs={{0,4},{8,0},{16,8},{24,16},{28,24},{20,28},{12,20},{4,12},{1,5},{9... | collective-permute-start | bytes 3538952 | tf_op jit(solution)/shard_map/ppermute | solution.py:229
  1090.9 47.8 %collective-permute-start.37 = (bf16[3,8,16,1536]{3,2,1,0:T(8,128)(2,1)S(1)}, bf16[3,8,16,1536]{3,2,1,0:T(8,128)(2,1)S(1)}, u32[]{:S(2)}, u32[]{:S(2)}) collective-permute-start(bf16[3,8,16,1536]{3,2,1,0:T(8,128)(2,1)S(1)} %copy-done.89), channel_id=1, source_target_pairs={{0,8},{8,16},{16,24},{24,28},{28,20},{20,12},{12,4},{4,0},{1,9},{9... | collective-permute-start | bytes 3538952 | tf_op jit(solution)/shard_map/ppermute | solution.py:229
  1091.7 47.5 %collective-permute-start.39 = (bf16[3,8,16,1536]{3,2,1,0:T(8,128)(2,1)S(1)}, bf16[3,8,16,1536]{3,2,1,0:T(8,128)(2,1)S(1)}, u32[]{:S(2)}, u32[]{:S(2)}) collective-permute-start(bf16[3,8,16,1536]{3,2,1,0:T(8,128)(2,1)S(1)} %copy-done.86), channel_id=1, source_target_pairs={{0,4},{8,0},{16,8},{24,16},{28,24},{20,28},{12,20},{4,12},{1,5},{9... | collective-permute-start | bytes 3538952 | tf_op jit(solution)/shard_map/ppermute | solution.py:229
  1097.6 155.7 %collective-permute-start.32 = (bf16[1024,1536]{1,0:T(8,128)(2,1)}, bf16[1024,1536]{1,0:T(8,128)(2,1)}, u32[]{:S(2)}, u32[]{:S(2)}) collective-permute-start(bf16[1024,1536]{1,0:T(8,128)(2,1)} %slice.761), channel_id=1, source_target_pairs={{0,2},{2,0},{1,3},{3,1},{4,6},{6,4},{5,7},{7,5},{8,10},{10,8},{9,1... | collective-permute-start | bytes 9437192 | tf_op jit(solution)/shard_map/ppermute | solution.py:153
  1156.3 177.9 %reduce-scatter.9.cloned.1.call-start = ((), (), s32[]{:S(2)}) async-start(), calls=%async_computation.9 | async-start | bytes 4595712
  1221.2 89.2 %collective-permute-start.54 = (bf16[3,8,16,1536]{3,2,1,0:T(8,128)(2,1)}, bf16[3,8,16,1536]{3,2,1,0:T(8,128)(2,1)}, u32[]{:S(2)}, u32[]{:S(2)}) collective-permute-start(bf16[3,8,16,1536]{3,2,1,0:T(8,128)(2,1)} %get-tuple-element.201), channel_id=1, source_target_pairs={{0,4},{8,0},{16,8},{24,16},{28,24},{20,28},{12,20},{4,12},{1,5},{9... | collective-permute-start | bytes 3538952 | tf_op jit(solution)/shard_map/ppermute | solution.py:229
  1224.2 65.0 %collective-permute-start.52 = (bf16[3,8,16,1536]{3,2,1,0:T(8,128)(2,1)}, bf16[3,8,16,1536]{3,2,1,0:T(8,128)(2,1)}, u32[]{:S(2)}, u32[]{:S(2)}) collective-permute-start(bf16[3,8,16,1536]{3,2,1,0:T(8,128)(2,1)} %get-tuple-element.200), channel_id=1, source_target_pairs={{0,8},{8,16},{16,24},{24,28},{28,20},{20,12},{12,4},{4,0},{1,9},{9... | collective-permute-start | bytes 3538952 | tf_op jit(solution)/shard_map/ppermute | solution.py:229
  1237.7 48.6 %collective-permute-start.51 = (bf16[3,8,16,1536]{3,2,1,0:T(8,128)(2,1)}, bf16[3,8,16,1536]{3,2,1,0:T(8,128)(2,1)}, u32[]{:S(2)}, u32[]{:S(2)}) collective-permute-start(bf16[3,8,16,1536]{3,2,1,0:T(8,128)(2,1)} %fusion.58), channel_id=1, source_target_pairs={{0,4},{8,0},{16,8},{24,16},{28,24},{20,28},{12,20},{4,12},{1,5},{9... | collective-permute-start | bytes 3538952 | tf_op jit(solution)/shard_map/ppermute | solution.py:229
  (193 other events, 3213.0 us)
Sparse Core Ops, SparseCore 0:
  11.8 66.3 all-gather.6
  79.7 97.6 all-gather.8
  178.9 98.8 all-gather.10
  279.3 98.8 all-gather.12
  379.6 98.8 all-gather.14
  479.9 98.8 all-gather.16
  1156.4 78.4 reduce-scatter.6
  1242.7 80.1 reduce-scatter.8

commit v2 on v1

--- a/solution.py
+++ b/solution.py
@@ -21,9 +21,10 @@
     (),
     ((0, 1), (1, 1), (2, 1)),
     ((0, 1), (1, 1), (2, 1), (3, 1), (4, 1)),
+    ((0, 1), (1, 1)),
     ((0, 1), (1, 1), (2, 1), (3, 1), (4, 1)),
-    ((0, 1), (1, 1), (3, 1)),
-    ((2, 1), (3, 1), (4, 2)),
+    ((2, 1), (3, 1), (4, 1)),
+    ((3, 1), (4, 1)),
 )
 BLOCK = 256
 RING = (0, 2, 4, 6, 7, 5, 3, 1)
@@ -564,7 +565,7 @@
             run_hops(expert_sums, g - 1)
             token_rows_g, cot_rows_g, mixture, rows_grad, grads, gathered[g] = tie(
                 (token_rows, cot_rows, mixture, rows_grad, grads, gathered[g]),
-                [expert_sums[done] for done, _ in HOPS[g - 1]],
+                expert_sums,
             )
             expert_sums.append(scatter_experts(grads, g - 1, starts))
         by_core = gathered[g].reshape(3, each, -1, 2, shard, D)
@@ -588,7 +589,7 @@
         gate_grads.append(gate_grad)
     run_hops(expert_sums, groups - 1)
     mixture, rows_grad, grads = tie(
-        (mixture, rows_grad, grads), [expert_sums[done] for done, _ in HOPS[groups - 1]]
+        (mixture, rows_grad, grads), expert_sums
     )
     expert_sums.append(scatter_experts(grads, groups - 1, starts))
     gate_grad_own = scatter_rows(jnp.concatenate(gate_grads, axis=1))
@@ -638,7 +639,11 @@
     else:
         mid_all = gather_ordered(mid_grad.astype(jnp.bfloat16))
     run_hops(expert_sums, groups)
-    mid_all, mixture = tie((mid_all, mixture), expert_sums)
+    run_hops(expert_sums, groups + 1)
+    crossing = [which for which, _ in HOPS[groups + 1]]
+    mid_all, mixture = tie(
+        (mid_all, mixture), [ring for k, ring in enumerate(expert_sums) if k not in crossing]
+    )
     mixed = swap(mixture[seq_len:].astype(jnp.bfloat16), "core")
     mixed = (mixture[:seq_len] + mixed.astype(jnp.float32)).astype(jnp.bfloat16)
     mixed = scatter_tensor(mixed, False)
@@ -663,7 +668,7 @@
     query_grad, key_grad, value_grad = attention_backward(
         query_rot, key_rot, value_hd, log_total, attn_out_grad
     )
-    run_hops(expert_sums, groups + 1)
+    run_hops(expert_sums, groups + 2)
     query_grad, key_grad, value_grad = tie((query_grad, key_grad, value_grad), expert_sums)
     query_pg = unrotate(query_grad, cosine, sine).reshape(seq_len, -1).astype(jnp.bfloat16)
     key_pg = unrotate(key_grad, cosine, sine).reshape(seq_len, -1).astype(jnp.bfloat16)
@@ -685,12 +690,11 @@
         ],
         axis=1,
     )
-    run_hops(expert_sums, groups + 2)
-    late = tie(late, expert_sums)
+    run_hops(expert_sums, groups + 3)
     late = lax.psum_scatter(late, ("chip", "core"), scatter_dimension=0, tiled=True).astype(
         jnp.float32
     )
-    run_hops(expert_sums, groups + 3)
+    run_hops(expert_sums, groups + 4)
     shared = early[:, q_cols:] + late[:, proj_cols:]
     if parts == 2:
         shared = shared + swap(shared, "tensor")

time: 1360 us -> 1320 us (0.971)
    ppermute x35, waiting for transfers between devices: 302 us -> 269 us  [send(): return lax.ppermute(block, 'chip', pairs)]
    unnamed x10, waiting for transfers between devices: 0.13 us -> 24.1 us
    all_gather x5, waiting for transfers between devices: 37.4 us -> 13.9 us  [body(): gathered.append(lax.all_gather(part, ('chip', 'core'), axis=2, tiled=True))]
    ppermute x20, waiting for transfers between devices: 95.9 us -> 115 us  [swap(): return lax.ppermute(values, axis, [(0, 1), (1, 0)])]
    unnamed x374 -> x328, local copies, waits for them, and re-layouts: 71.7 us -> 64 us
  transfers between devices with their start and end apart: 63 -> 63, of which waited for: 32 -> 32; matrix products, arithmetic and copies ran while one was open for 22% -> 23% of each run, Pallas kernels for 24% -> 30%
where the time goes in v2:
time: 1320 us; the launch traced here: 1310 us
  waiting for transfers between devices  429 us (32%)
  Pallas kernels  400 us (30%)
  other arithmetic  157 us (12%)
  matrix products  118 us (9%)
  local copies, waits for them, and re-layouts  116 us (9%)
  starting transfers between devices  59.3 us (4%)
  between operations  31.8 us (2%)
    pallas_call x5, Pallas kernels, expert_call(): pl.pallas_call(functools.partial(expert_kernel, first), grid_spec=pltpu.P...  400 us
    ppermute x35, waiting for transfers between devices, send(): return lax.ppermute(block, 'chip', pairs)  269 us
    ppermute x20, waiting for transfers between devices, swap(): return lax.ppermute(values, axis, [(0, 1), (1, 0)])  115 us
    unnamed x328, local copies, waits for them, and re-layouts  64 us
    convert_element_type x15, other arithmetic, add(): (block.astype(jnp.float32) + own.astype(jnp.float32)).astype(jnp.bfloat16)  51.4 us
    ppermute x35, starting transfers between devices, send(): return lax.ppermute(block, 'chip', pairs)  41.6 us
  transfers between devices with their start and end apart: 63, of which 32 were waited for; matrix products, arithmetic and copies ran while one was open for 23% of the time, Pallas kernels for 30%

profile of v2, /device:TPU:0, one launch (start us, length us, event | category | flops | bytes accessed | tf_op | source)
XLA Modules:
  0.0 1310.4 jit_solution(15235163863410425138)
XLA Ops:
  31.6 31.4 %collective-permute-done = bf16[512,1536]{1,0:T(8,128)(2,1)} collective-permute-done((bf16[512,1536]{1,0:T(8,128)(2,1)S(1)}, bf16[512,1536]{1,0:T(8,128)(2,1)}, u32[]{:S(2)}, u32[]{:S(2)}) %collective-permute-start) | collective-permute-done | bytes 1572896 | tf_op jit(solution)/shard_map/ppermute | solution.py:154
  70.8 7.4 all-gather.7.cloned.1.call-done
  133.3 8.3 collective-permute-done.2
  141.6 16.0 %collective-permute-done.1 = bf16[256,1536]{1,0:T(8,128)(2,1)} collective-permute-done((bf16[256,1536]{1,0:T(8,128)(2,1)}, bf16[256,1536]{1,0:T(8,128)(2,1)}, u32[]{:S(2)}, u32[]{:S(2)}) %collective-permute-start.1) | collective-permute-done | bytes 786464 | tf_op jit(solution)/shard_map/ppermute | solution.py:154
  185.2 15.2 %collective-permute-done.3 = bf16[256,1536]{1,0:T(8,128)(2,1)} collective-permute-done((bf16[256,1536]{1,0:T(8,128)(2,1)}, bf16[256,1536]{1,0:T(8,128)(2,1)}, u32[]{:S(2)}, u32[]{:S(2)}) %collective-permute-start.3) | collective-permute-done | bytes 786464 | tf_op jit(solution)/shard_map/ppermute | solution.py:154
  215.6 6.4 fusion.144
  234.5 80.3 %experts.5 = (f32[2048,1536]{1,0:T(8,128)}, f32[2048,1536]{1,0:T(8,128)}, f32[4,2,2048]{2,1,0:T(2,128)}, bf16[8,3,8,16,1536]{4,3,2,1,0:T(8,128)(2,1)}) custom-call(s32[1]{0:T(128)} %bitcast.40.core_ref, bf16[2048,1536]{1,0:T(8,128)(2,1)} %copy-done.17, bf16[2048,1536]{1,0:T(8,128)(2,1)} %copy-done.78, f32[4,2,2048]{2,1,0:T(2,128)} %reshape.481.gates_ref, ...), custom_call_target="tpu_custom_call" | custom-call | flops 57982058496 | bytes 69206016 | tf_op jit(solution)/shard_map/experts/pallas_call | solution.py:397
  318.2 79.7 %experts.6 = (f32[2048,1536]{1,0:T(8,128)}, f32[2048,1536]{1,0:T(8,128)}, f32[4,2,2048]{2,1,0:T(2,128)}, bf16[8,3,8,16,1536]{4,3,2,1,0:T(8,128)(2,1)}) custom-call(s32[1]{0:T(128)} %bitcast.40.core_ref, bf16[2048,1536]{1,0:T(8,128)(2,1)} %copy-done.17, bf16[2048,1536]{1,0:T(8,128)(2,1)} %copy-done.78, ...), custom_call_target="tpu_custom_call", output_to_operand_aliasing={{0}: (5, {}), {1}: (6, {})} | custom-call | flops 57982058496 | bytes 69206016 | tf_op jit(solution)/shard_map/experts/pallas_call | solution.py:397
  401.4 79.8 %experts.7 = (f32[2048,1536]{1,0:T(8,128)}, f32[2048,1536]{1,0:T(8,128)}, f32[4,2,2048]{2,1,0:T(2,128)}, bf16[8,3,8,16,1536]{4,3,2,1,0:T(8,128)(2,1)}) custom-call(s32[1]{0:T(128)} %bitcast.40.core_ref, bf16[2048,1536]{1,0:T(8,128)(2,1)} %copy-done.17, bf16[2048,1536]{1,0:T(8,128)(2,1)} %copy-done.78, ...), custom_call_target="tpu_custom_call", output_to_operand_aliasing={{0}: (5, {}), {1}: (6, {})} | custom-call | flops 57982058496 | bytes 69206016 | tf_op jit(solution)/shard_map/experts/pallas_call | solution.py:397
  484.5 80.4 %experts.8 = (f32[2048,1536]{1,0:T(8,128)}, f32[2048,1536]{1,0:T(8,128)}, f32[4,2,2048]{2,1,0:T(2,128)}, bf16[8,3,8,16,1536]{4,3,2,1,0:T(8,128)(2,1)}) custom-call(s32[1]{0:T(128)} %bitcast.40.core_ref, bf16[2048,1536]{1,0:T(8,128)(2,1)} %copy-done.17, bf16[2048,1536]{1,0:T(8,128)(2,1)} %copy-done.78, ...), custom_call_target="tpu_custom_call", output_to_operand_aliasing={{0}: (5, {}), {1}: (6, {})} | custom-call | flops 57982058496 | bytes 69206016 | tf_op jit(solution)/shard_map/experts/pallas_call | solution.py:397
  565.0 13.9 %all-gather.17.cloned.1.call-done = bf16[3,8,256,1536]{3,2,1,0:T(8,128)(2,1)} async-done(((bf16[3,8,16,1536]{3,2,1,0:T(8,128)(2,1)}), bf16[3,8,256,1536]{3,2,1,0:T(8,128)(2,1)}) %all-gather.17.cloned.1.call-update) | async-done | bytes 18874384 | tf_op jit(solution)/shard_map/all_gather | solution.py:515
  588.7 79.3 %experts.9 = (f32[2048,1536]{1,0:T(8,128)}, f32[2048,1536]{1,0:T(8,128)}, f32[4,2,2048]{2,1,0:T(2,128)}, bf16[8,3,8,16,1536]{4,3,2,1,0:T(8,128)(2,1)}) custom-call(s32[1]{0:T(128)} %bitcast.40.core_ref, bf16[2048,1536]{1,0:T(8,128)(2,1)} %copy-done.17, bf16[2048,1536]{1,0:T(8,128)(2,1)} %copy-done.78, ...), custom_call_target="tpu_custom_call", output_to_operand_aliasing={{0}: (5, {}), {1}: (6, {})} | custom-call | flops 57982058496 | bytes 69206016 | tf_op jit(solution)/shard_map/experts/pallas_call | solution.py:397
  682.6 17.9 %collective-permute-done.12 = bf16[3,8,16,1536]{3,2,1,0:T(8,128)(2,1)S(1)} collective-permute-done((bf16[3,8,16,1536]{3,2,1,0:T(8,128)(2,1)}, bf16[3,8,16,1536]{3,2,1,0:T(8,128)(2,1)S(1)}, u32[]{:S(2)}, u32[]{:S(2)}) %collective-permute-start.12) | collective-permute-done | bytes 1179680 | tf_op jit(solution)/shard_map/ppermute | solution.py:230
  718.3 14.8 %collective-permute-done.35 = bf16[3,8,16,1536]{3,2,1,0:T(8,128)(2,1)S(1)} collective-permute-done((bf16[3,8,16,1536]{3,2,1,0:T(8,128)(2,1)S(1)}, bf16[3,8,16,1536]{3,2,1,0:T(8,128)(2,1)S(1)}, u32[]{:S(2)}, u32[]{:S(2)}) %collective-permute-start.35) | collective-permute-done | bytes 1179680 | tf_op jit(solution)/shard_map/ppermute | solution.py:230
  744.1 14.3 %collective-permute-done.27 = bf16[3,8,16,1536]{3,2,1,0:T(8,128)(2,1)S(1)} collective-permute-done((bf16[3,8,16,1536]{3,2,1,0:T(8,128)(2,1)S(1)}, bf16[3,8,16,1536]{3,2,1,0:T(8,128)(2,1)S(1)}, u32[]{:S(2)}, u32[]{:S(2)}) %collective-permute-start.27) | collective-permute-done | bytes 1179680 | tf_op jit(solution)/shard_map/ppermute | solution.py:230
  762.2 21.5 %collective-permute-done.24 = bf16[3,8,16,1536]{3,2,1,0:T(8,128)(2,1)S(1)} collective-permute-done((bf16[3,8,16,1536]{3,2,1,0:T(8,128)(2,1)S(1)}, bf16[3,8,16,1536]{3,2,1,0:T(8,128)(2,1)S(1)}, u32[]{:S(2)}, u32[]{:S(2)}) %collective-permute-start.24) | collective-permute-done | bytes 1179680 | tf_op jit(solution)/shard_map/ppermute | solution.py:230
  795.6 13.4 %collective-permute-done.23 = bf16[3,8,16,1536]{3,2,1,0:T(8,128)(2,1)S(1)} collective-permute-done((bf16[3,8,16,1536]{3,2,1,0:T(8,128)(2,1)S(1)}, bf16[3,8,16,1536]{3,2,1,0:T(8,128)(2,1)S(1)}, u32[]{:S(2)}, u32[]{:S(2)}) %collective-permute-start.23) | collective-permute-done | bytes 1179680 | tf_op jit(solution)/shard_map/ppermute | solution.py:230
  819.9 24.3 %collective-permute-done.30 = bf16[3,8,16,1536]{3,2,1,0:T(8,128)(2,1)S(1)} collective-permute-done((bf16[3,8,16,1536]{3,2,1,0:T(8,128)(2,1)}, bf16[3,8,16,1536]{3,2,1,0:T(8,128)(2,1)S(1)}, u32[]{:S(2)}, u32[]{:S(2)}) %collective-permute-start.30) | collective-permute-done | bytes 1179680 | tf_op jit(solution)/shard_map/ppermute | solution.py:230
  847.2 9.4 collective-permute-done.36
  880.8 8.2 collective-permute-done.20
  889.0 14.7 %collective-permute-done.21 = bf16[256,1536]{1,0:T(8,128)(2,1)S(1)} collective-permute-done((bf16[256,1536]{1,0:T(8,128)(2,1)S(1)}, bf16[256,1536]{1,0:T(8,128)(2,1)S(1)}, u32[]{:S(2)}, u32[]{:S(2)}) %collective-permute-start.21) | collective-permute-done | bytes 786464 | tf_op jit(solution)/shard_map/ppermute | solution.py:154
  932.1 10.6 fusion.9
  983.5 8.9 fusion.109
  1003.2 38.5 %collective-permute-done.40 = bf16[3,8,16,1536]{3,2,1,0:T(8,128)(2,1)} collective-permute-done((bf16[3,8,16,1536]{3,2,1,0:T(8,128)(2,1)}, bf16[3,8,16,1536]{3,2,1,0:T(8,128)(2,1)}, u32[]{:S(2)}, u32[]{:S(2)}) %collective-permute-start.40) | collective-permute-done | bytes 1179680 | tf_op jit(solution)/shard_map/ppermute | solution.py:230
  1059.9 16.3 %collective-permute-done.37 = bf16[3,8,16,1536]{3,2,1,0:T(8,128)(2,1)S(1)} collective-permute-done((bf16[3,8,16,1536]{3,2,1,0:T(8,128)(2,1)S(1)}, bf16[3,8,16,1536]{3,2,1,0:T(8,128)(2,1)S(1)}, u32[]{:S(2)}, u32[]{:S(2)}) %collective-permute-start.37) | collective-permute-done | bytes 1179680 | tf_op jit(solution)/shard_map/ppermute | solution.py:230
  1076.6 22.6 %collective-permute-done.32 = bf16[3,8,16,1536]{3,2,1,0:T(8,128)(2,1)S(1)} collective-permute-done((bf16[3,8,16,1536]{3,2,1,0:T(8,128)(2,1)S(1)}, bf16[3,8,16,1536]{3,2,1,0:T(8,128)(2,1)S(1)}, u32[]{:S(2)}, u32[]{:S(2)}) %collective-permute-start.32) | collective-permute-done | bytes 1179680 | tf_op jit(solution)/shard_map/ppermute | solution.py:230
  1101.5 22.4 %collective-permute-done.41 = bf16[3,8,16,1536]{3,2,1,0:T(8,128)(2,1)S(1)} collective-permute-done((bf16[3,8,16,1536]{3,2,1,0:T(8,128)(2,1)S(1)}, bf16[3,8,16,1536]{3,2,1,0:T(8,128)(2,1)S(1)}, u32[]{:S(2)}, u32[]{:S(2)}) %collective-permute-start.41) | collective-permute-done | bytes 1179680 | tf_op jit(solution)/shard_map/ppermute | solution.py:230
  1149.2 6.7 convolution_convert_fusion
  1168.8 35.9 %collective-permute-done.52 = bf16[3,8,16,1536]{3,2,1,0:T(8,128)(2,1)S(1)} collective-permute-done((bf16[3,8,16,1536]{3,2,1,0:T(8,128)(2,1)S(1)}, bf16[3,8,16,1536]{3,2,1,0:T(8,128)(2,1)S(1)}, u32[]{:S(2)}, u32[]{:S(2)}) %collective-permute-start.52) | collective-permute-done | bytes 1179680 | tf_op jit(solution)/shard_map/ppermute | solution.py:230
  1215.1 6.5 copy.227
  1252.4 15.8 %collective-permute-done.29 = bf16[512,1536]{1,0:T(8,128)(2,1)} collective-permute-done((bf16[512,1536]{1,0:T(8,128)(2,1)}, bf16[512,1536]{1,0:T(8,128)(2,1)}, u32[]{:S(2)}, u32[]{:S(2)}) %collective-permute-start.29) | collective-permute-done | bytes 1572896 | tf_op jit(solution)/shard_map/ppermute | solution.py:154
  1271.9 23.9 %reduce-scatter.9.cloned.1.call-done = bf16[96,1408]{1,0:T(8,128)(2,1)} async-done(((bf16[1536,1408]{1,0:T(8,128)(2,1)}), bf16[96,1408]{1,0:T(8,128)(2,1)}) %reduce-scatter.9.cloned.1.call-update) | async-done | bytes 270352
  (645 shorter events, 434.2 us)
Async XLA Ops:
  7.2 71.0 %all-gather.7.cloned.1.call-start = ((), (), s32[]{:S(2)}) async-start(), calls=%async_computation.2 | async-start | bytes 7102464 | tf_op jit(solution)/shard_map/all_gather | solution.py:500
  11.6 222.9 %all-gather.9.cloned.1.call-start = ((), (), s32[]{:S(2)}) async-start(), calls=%async_computation.3 | async-start | bytes 20054016 | tf_op jit(solution)/shard_map/all_gather | solution.py:515
  18.3 296.5 %all-gather.11.cloned.1.call-start = ((), (), s32[]{:S(2)}) async-start(), calls=%async_computation.4 | async-start | bytes 20054016 | tf_op jit(solution)/shard_map/all_gather | solution.py:515
  21.0 376.9 %all-gather.13.cloned.1.call-start = ((), (), s32[]{:S(2)}) async-start(), calls=%async_computation.5 | async-start | bytes 20054016 | tf_op jit(solution)/shard_map/all_gather | solution.py:515
  22.6 458.7 %all-gather.15.cloned.1.call-start = ((), (), s32[]{:S(2)}) async-start(), calls=%async_computation.6 | async-start | bytes 20054016 | tf_op jit(solution)/shard_map/all_gather | solution.py:515
  25.5 553.4 %all-gather.17.cloned.1.call-start = ((), (), s32[]{:S(2)}) async-start(), calls=%async_computation.7 | async-start | bytes 20054016 | tf_op jit(solution)/shard_map/all_gather | solution.py:515
  30.0 1219.6 %reduce-scatter.7.cloned.1.call-start = ((), (), s32[]{:S(2)}) async-start(), calls=%async_computation.8 | async-start | bytes 2924544
  69.0 59.9 %collective-permute-start.6 = (bf16[512,1536]{1,0:T(8,128)(2,1)}, bf16[512,1536]{1,0:T(8,128)(2,1)}, u32[]{:S(2)}, u32[]{:S(2)}) collective-permute-start(bf16[512,1536]{1,0:T(8,128)(2,1)} %param.26), channel_id=1, source_target_pairs={{0,1},{1,0},{2,3},{3,2},{4,5},{5,4},{6,7},{7,6},{8,9},{9,8},{10,11... | collective-permute-start | bytes 4718600 | tf_op jit(solution)/shard_map/ppermute | solution.py:154
  127.4 56.2 %collective-permute-start.8 = (s32[1024,8]{0,1:T(8,128)S(1)}, s32[1024,8]{0,1:T(8,128)S(1)}, u32[]{:S(2)}, u32[]{:S(2)}) collective-permute-start(s32[1024,8]{0,1:T(8,128)S(1)} %pad_add_fusion.1), channel_id=1, source_target_pairs={{0,2},{2,0},{1,3},{3,1},{4,6},{6,4},{5,7},{7,5},{8,10},{10,8},{9,1... | collective-permute-start | bytes 98312 | tf_op jit(solution)/shard_map/ppermute | solution.py:154
  132.9 73.6 %collective-permute-start.7 = (bf16[1024,1536]{1,0:T(8,128)(2,1)}, bf16[1024,1536]{1,0:T(8,128)(2,1)}, u32[]{:S(2)}, u32[]{:S(2)}) collective-permute-start(bf16[1024,1536]{1,0:T(8,128)(2,1)} %pad_maximum_fusion.3), channel_id=1, source_target_pairs={{0,2},{2,0},{1,3},{3,1},{4,6},{6,4},{5,7},{7,5},{8,10},{10,8},{9,1... | collective-permute-start | bytes 9437192 | tf_op jit(solution)/shard_map/ppermute | solution.py:154
  578.8 94.3 %collective-permute-start.13 = (bf16[3,8,16,1536]{3,2,1,0:T(8,128)(2,1)}, bf16[3,8,16,1536]{3,2,1,0:T(8,128)(2,1)}, u32[]{:S(2)}, u32[]{:S(2)}) collective-permute-start(bf16[3,8,16,1536]{3,2,1,0:T(8,128)(2,1)} %get-tuple-element.160), channel_id=1, source_target_pairs={{0,8},{8,16},{16,24},{24,28},{28,20},{20,12},{12,4},{4,0},{1,9},{9... | collective-permute-start | bytes 3538952 | tf_op jit(solution)/shard_map/ppermute | solution.py:230
  580.3 94.0 %collective-permute-start.14 = (bf16[3,8,16,1536]{3,2,1,0:T(8,128)(2,1)}, bf16[3,8,16,1536]{3,2,1,0:T(8,128)(2,1)}, u32[]{:S(2)}, u32[]{:S(2)}) collective-permute-start(bf16[3,8,16,1536]{3,2,1,0:T(8,128)(2,1)} %get-tuple-element.161), channel_id=1, source_target_pairs={{0,4},{8,0},{16,8},{24,16},{28,24},{20,28},{12,20},{4,12},{1,5},{9... | collective-permute-start | bytes 3538952 | tf_op jit(solution)/shard_map/ppermute | solution.py:230
  580.9 101.7 %collective-permute-start.11 = (bf16[3,8,16,1536]{3,2,1,0:T(8,128)(2,1)}, bf16[3,8,16,1536]{3,2,1,0:T(8,128)(2,1)}, u32[]{:S(2)}, u32[]{:S(2)}) collective-permute-start(bf16[3,8,16,1536]{3,2,1,0:T(8,128)(2,1)} %get-tuple-element.158), channel_id=1, source_target_pairs={{0,4},{8,0},{16,8},{24,16},{28,24},{20,28},{12,20},{4,12},{1,5},{9... | collective-permute-start | bytes 3538952 | tf_op jit(solution)/shard_map/ppermute | solution.py:230
  582.1 95.6 %collective-permute-start.10 = (bf16[3,8,16,1536]{3,2,1,0:T(8,128)(2,1)}, bf16[3,8,16,1536]{3,2,1,0:T(8,128)(2,1)}, u32[]{:S(2)}, u32[]{:S(2)}) collective-permute-start(bf16[3,8,16,1536]{3,2,1,0:T(8,128)(2,1)} %get-tuple-element.157), channel_id=1, source_target_pairs={{0,4},{8,0},{16,8},{24,16},{28,24},{20,28},{12,20},{4,12},{1,5},{9... | collective-permute-start | bytes 3538952 | tf_op jit(solution)/shard_map/ppermute | solution.py:230
  583.6 94.1 %collective-permute-start.9 = (bf16[3,8,16,1536]{3,2,1,0:T(8,128)(2,1)}, bf16[3,8,16,1536]{3,2,1,0:T(8,128)(2,1)}, u32[]{:S(2)}, u32[]{:S(2)}) collective-permute-start(bf16[3,8,16,1536]{3,2,1,0:T(8,128)(2,1)} %get-tuple-element.156), channel_id=1, source_target_pairs={{0,8},{8,16},{16,24},{24,28},{28,20},{20,12},{12,4},{4,0},{1,9},{9... | collective-permute-start | bytes 3538952 | tf_op jit(solution)/shard_map/ppermute | solution.py:230
  714.3 99.9 %collective-permute-start.15 = (bf16[1024,1536]{1,0:T(8,128)(2,1)S(1)}, bf16[1024,1536]{1,0:T(8,128)(2,1)S(1)}, u32[]{:S(2)}, u32[]{:S(2)}) collective-permute-start(bf16[1024,1536]{1,0:T(8,128)(2,1)S(1)} %slice.762), channel_id=1, source_target_pairs={{0,2},{2,0},{1,3},{3,1},{4,6},{6,4},{5,7},{7,5},{8,10},{10,8},{9,1... | collective-permute-start | bytes 9437192 | tf_op jit(solution)/shard_map/ppermute | solution.py:154
  716.8 66.9 %collective-permute-start.24 = (bf16[3,8,16,1536]{3,2,1,0:T(8,128)(2,1)S(1)}, bf16[3,8,16,1536]{3,2,1,0:T(8,128)(2,1)S(1)}, u32[]{:S(2)}, u32[]{:S(2)}) collective-permute-start(bf16[3,8,16,1536]{3,2,1,0:T(8,128)(2,1)S(1)} %copy-done.69), channel_id=1, source_target_pairs={{0,4},{8,0},{16,8},{24,16},{28,24},{20,28},{12,20},{4,12},{1,5},{9... | collective-permute-start | bytes 3538952 | tf_op jit(solution)/shard_map/ppermute | solution.py:230
  783.7 62.7 %collective-permute-start.38 = (bf16[3,8,16,1536]{3,2,1,0:T(8,128)(2,1)}, bf16[3,8,16,1536]{3,2,1,0:T(8,128)(2,1)}, u32[]{:S(2)}, u32[]{:S(2)}) collective-permute-start(bf16[3,8,16,1536]{3,2,1,0:T(8,128)(2,1)} %get-tuple-element.180), channel_id=1, source_target_pairs={{0,8},{8,16},{16,24},{24,28},{28,20},{20,12},{12,4},{4,0},{1,9},{9... | collective-permute-start | bytes 3538952 | tf_op jit(solution)/shard_map/ppermute | solution.py:230
  784.4 59.7 %collective-permute-start.30 = (bf16[3,8,16,1536]{3,2,1,0:T(8,128)(2,1)}, bf16[3,8,16,1536]{3,2,1,0:T(8,128)(2,1)S(1)}, u32[]{:S(2)}, u32[]{:S(2)}) collective-permute-start(bf16[3,8,16,1536]{3,2,1,0:T(8,128)(2,1)} %get-tuple-element.177), channel_id=1, source_target_pairs={{0,8},{8,16},{16,24},{24,28},{28,20},{20,12},{12,4},{4,0},{1,9},{9... | collective-permute-start | bytes 3538952 | tf_op jit(solution)/shard_map/ppermute | solution.py:230
  794.1 76.5 %collective-permute-start.33 = (bf16[3,8,16,1536]{3,2,1,0:T(8,128)(2,1)}, bf16[3,8,16,1536]{3,2,1,0:T(8,128)(2,1)}, u32[]{:S(2)}, u32[]{:S(2)}) collective-permute-start(bf16[3,8,16,1536]{3,2,1,0:T(8,128)(2,1)} %get-tuple-element.178), channel_id=1, source_target_pairs={{0,4},{8,0},{16,8},{24,16},{28,24},{20,28},{12,20},{4,12},{1,5},{9... | collective-permute-start | bytes 3538952 | tf_op jit(solution)/shard_map/ppermute | solution.py:230
  955.8 91.5 %collective-permute-start.44 = (bf16[3,8,16,1536]{3,2,1,0:T(8,128)(2,1)}, bf16[3,8,16,1536]{3,2,1,0:T(8,128)(2,1)}, u32[]{:S(2)}, u32[]{:S(2)}) collective-permute-start(bf16[3,8,16,1536]{3,2,1,0:T(8,128)(2,1)} %get-tuple-element.185), channel_id=1, source_target_pairs={{0,8},{8,16},{16,24},{24,28},{28,20},{20,12},{12,4},{4,0},{1,9},{9... | collective-permute-start | bytes 3538952 | tf_op jit(solution)/shard_map/ppermute | solution.py:230
  956.4 91.0 %collective-permute-start.45 = (bf16[3,8,16,1536]{3,2,1,0:T(8,128)(2,1)}, bf16[3,8,16,1536]{3,2,1,0:T(8,128)(2,1)}, u32[]{:S(2)}, u32[]{:S(2)}) collective-permute-start(bf16[3,8,16,1536]{3,2,1,0:T(8,128)(2,1)} %get-tuple-element.186), channel_id=1, source_target_pairs={{0,4},{8,0},{16,8},{24,16},{28,24},{20,28},{12,20},{4,12},{1,5},{9... | collective-permute-start | bytes 3538952 | tf_op jit(solution)/shard_map/ppermute | solution.py:230
  957.8 90.6 %collective-permute-start.42 = (bf16[3,8,16,1536]{3,2,1,0:T(8,128)(2,1)}, bf16[3,8,16,1536]{3,2,1,0:T(8,128)(2,1)}, u32[]{:S(2)}, u32[]{:S(2)}) collective-permute-start(bf16[3,8,16,1536]{3,2,1,0:T(8,128)(2,1)} %get-tuple-element.183), channel_id=1, source_target_pairs={{0,4},{8,0},{16,8},{24,16},{28,24},{20,28},{12,20},{4,12},{1,5},{9... | collective-permute-start | bytes 3538952 | tf_op jit(solution)/shard_map/ppermute | solution.py:230
  959.3 90.1 %collective-permute-start.43 = (bf16[3,8,16,1536]{3,2,1,0:T(8,128)(2,1)}, bf16[3,8,16,1536]{3,2,1,0:T(8,128)(2,1)}, u32[]{:S(2)}, u32[]{:S(2)}) collective-permute-start(bf16[3,8,16,1536]{3,2,1,0:T(8,128)(2,1)} %get-tuple-element.184), channel_id=1, source_target_pairs={{0,8},{8,16},{16,24},{24,28},{28,20},{20,12},{12,4},{4,0},{1,9},{9... | collective-permute-start | bytes 3538952 | tf_op jit(solution)/shard_map/ppermute | solution.py:230
  959.9 81.8 %collective-permute-start.40 = (bf16[3,8,16,1536]{3,2,1,0:T(8,128)(2,1)}, bf16[3,8,16,1536]{3,2,1,0:T(8,128)(2,1)}, u32[]{:S(2)}, u32[]{:S(2)}) collective-permute-start(bf16[3,8,16,1536]{3,2,1,0:T(8,128)(2,1)} %get-tuple-element.181), channel_id=1, source_target_pairs={{0,8},{8,16},{16,24},{24,28},{28,20},{20,12},{12,4},{4,0},{1,9},{9... | collective-permute-start | bytes 3538952 | tf_op jit(solution)/shard_map/ppermute | solution.py:230
  980.7 315.1 %reduce-scatter.9.cloned.1.call-start = ((), (), s32[]{:S(2)}) async-start(), calls=%async_computation.9 | async-start | bytes 4595712
  1048.5 53.0 %collective-permute-start.34 = (bf16[3,8,16,1536]{3,2,1,0:T(8,128)(2,1)S(1)}, bf16[3,8,16,1536]{3,2,1,0:T(8,128)(2,1)S(1)}, u32[]{:S(2)}, u32[]{:S(2)}) collective-permute-start(bf16[3,8,16,1536]{3,2,1,0:T(8,128)(2,1)S(1)} %copy-done.73), channel_id=1, source_target_pairs={{0,4},{8,0},{16,8},{24,16},{28,24},{20,28},{12,20},{4,12},{1,5},{9... | collective-permute-start | bytes 3538952 | tf_op jit(solution)/shard_map/ppermute | solution.py:230
  1049.5 74.4 %collective-permute-start.41 = (bf16[3,8,16,1536]{3,2,1,0:T(8,128)(2,1)S(1)}, bf16[3,8,16,1536]{3,2,1,0:T(8,128)(2,1)S(1)}, u32[]{:S(2)}, u32[]{:S(2)}) collective-permute-start(bf16[3,8,16,1536]{3,2,1,0:T(8,128)(2,1)S(1)} %copy-done.70), channel_id=1, source_target_pairs={{0,4},{8,0},{16,8},{24,16},{28,24},{20,28},{12,20},{4,12},{1,5},{9... | collective-permute-start | bytes 3538952 | tf_op jit(solution)/shard_map/ppermute | solution.py:230
  1076.2 151.9 %collective-permute-start.28 = (bf16[1024,1536]{1,0:T(8,128)(2,1)}, bf16[1024,1536]{1,0:T(8,128)(2,1)}, u32[]{:S(2)}, u32[]{:S(2)}) collective-permute-start(bf16[1024,1536]{1,0:T(8,128)(2,1)} %slice.761), channel_id=1, source_target_pairs={{0,2},{2,0},{1,3},{3,1},{4,6},{6,4},{5,7},{7,5},{8,10},{10,8},{9,1... | collective-permute-start | bytes 9437192 | tf_op jit(solution)/shard_map/ppermute | solution.py:154
  1131.1 103.6 %collective-permute-start.51 = (bf16[3,8,16,1536]{3,2,1,0:T(8,128)(2,1)}, bf16[3,8,16,1536]{3,2,1,0:T(8,128)(2,1)}, u32[]{:S(2)}, u32[]{:S(2)}) collective-permute-start(bf16[3,8,16,1536]{3,2,1,0:T(8,128)(2,1)} %get-tuple-element.197), channel_id=1, source_target_pairs={{0,8},{8,16},{16,24},{24,28},{28,20},{20,12},{12,4},{4,0},{1,9},{9... | collective-permute-start | bytes 3538952 | tf_op jit(solution)/shard_map/ppermute | solution.py:230
  1132.8 71.9 %collective-permute-start.52 = (bf16[3,8,16,1536]{3,2,1,0:T(8,128)(2,1)S(1)}, bf16[3,8,16,1536]{3,2,1,0:T(8,128)(2,1)S(1)}, u32[]{:S(2)}, u32[]{:S(2)}) collective-permute-start(bf16[3,8,16,1536]{3,2,1,0:T(8,128)(2,1)S(1)} %get-tuple-element.198), channel_id=1, source_target_pairs={{0,8},{8,16},{16,24},{24,28},{28,20},{20,12},{12,4},{4,0},{1,9},{9... | collective-permute-start | bytes 3538952 | tf_op jit(solution)/shard_map/ppermute | solution.py:230
  1164.8 73.9 %collective-permute-start.54 = (bf16[3,8,16,1536]{3,2,1,0:T(8,128)(2,1)}, bf16[3,8,16,1536]{3,2,1,0:T(8,128)(2,1)}, u32[]{:S(2)}, u32[]{:S(2)}) collective-permute-start(bf16[3,8,16,1536]{3,2,1,0:T(8,128)(2,1)} %get-tuple-element.199), channel_id=1, source_target_pairs={{0,4},{8,0},{16,8},{24,16},{28,24},{20,28},{12,20},{4,12},{1,5},{9... | collective-permute-start | bytes 3538952 | tf_op jit(solution)/shard_map/ppermute | solution.py:230
  (170 other events, 3150.3 us)
Sparse Core Ops, SparseCore 0:
  11.8 66.3 all-gather.6
  79.7 97.6 all-gather.8
  178.9 98.8 all-gather.10
  279.3 98.8 all-gather.12
  379.6 98.8 all-gather.14
  479.9 98.8 all-gather.16
  980.8 77.8 reduce-scatter.6
  1221.8 73.9 reduce-scatter.8
